TPU v7x, 32 devices: a whole 2x2x4 slice. The times are simulated.
32 devices in a mesh: fsdp: 4 (over x, core), ctx: 4 (over z), tp: 2 (over y).
Axes of the slice: x: 2, y: 2, z: 4, core: 2. Of those that a mesh axis runs over, the one named last changes fastest.
Arguments:
- x_in: bfloat16 [8, 1024, 768], P('fsdp', 'ctx'), may hold values from -6 to 6
- out_cot: bfloat16 [8, 1024, 768], P('fsdp', 'ctx'), may hold values from -6 to 6
- seg_ids: int32 [8, 1024], P('fsdp', 'ctx'), may hold values from 0 to 16, as said below
- land_doc: int32 [8, 64], P('fsdp', 'ctx'), may hold values from 0 to 16, as said below
- w_qkv: bfloat16 [768, 3, 768], P(('fsdp', 'ctx'), None, 'tp'), may hold values from -0.21875 to 0.21875
- w_out: bfloat16 [768, 768], P(('fsdp', 'ctx'), 'tp'), may hold values from -0.4375 to 0.4375
- w_up: bfloat16 [768, 3072], P(('fsdp', 'ctx'), 'tp'), may hold values from -0.21875 to 0.21875
- w_down: bfloat16 [768, 3072], P(('fsdp', 'ctx'), 'tp'), may hold values from -0.109375 to 0.109375
- conv_taps: float32 [33, 12], P(None, 'tp'), may hold values from -2 to 2
- head_bias: float32 [2, 768], P(None, 'tp'), may hold values from -6 to 6
- ffn_bias: float32 [3072], P('tp'), may hold values from -4 to 4
- gains: float32 [2, 768], replicated, may hold values from 0.5 to 1.5
- offsets: float32 [4, 768], replicated, may hold values from -4 to 4
Outputs:
- y_out: bfloat16 [8, 1024, 768], P('fsdp', 'ctx')
- x_grad: bfloat16 [8, 1024, 768], P('fsdp', 'ctx')
- w_qkv_grad: float32 [768, 3, 768], P(('fsdp', 'ctx'), None, 'tp')
- w_out_grad: float32 [768, 768], P(('fsdp', 'ctx'), 'tp')
- w_up_grad: float32 [768, 3072], P(('fsdp', 'ctx'), 'tp')
- w_down_grad: float32 [768, 3072], P(('fsdp', 'ctx'), 'tp')
- conv_grad: float32 [33, 12], P(None, 'tp')
- head_bias_grad: float32 [2, 768], P(None, 'tp')
- ffn_bias_grad: float32 [3072], P('tp')
- gains_grad: float32 [2, 768], replicated
- offsets_grad: float32 [4, 768], replicated
Inputs may be any that keep to these rules, and one draw needn't show every extreme that they name: `seg_ids`: within each sequence the ids start at 0, never fall and rise by one where a new document begins; every document covers 60 or more consecutive positions, so no id exceeds 1024 // 60 - 1, and some sequence reaches that id. `land_doc`: landmark j of a sequence carries the seg_ids of that sequence's position j * 16.
All inputs are finite; a program needn't handle non-finite values.
Results may differ from a plain program's by a relative error of at most 0.029.
Values may be sent and summed in bfloat16 or wider, within the bound.
No kernel may reach another device: no remote copies, remote signals or barrier semaphores. Data moves between devices by JAX's collectives and lax.ppermute only.
A program may use at most 128 MiB of HBM per device.

v0:
```python
import jax
import jax.numpy as jnp
from jax import lax
from jax.sharding import PartitionSpec as P

HEAD_DIM = 64
KW = 33
NEWTON = 6


highest_precision = lax.Precision.HIGHEST
epsilon = 1e-05


def with_halo(array, sides, width):
    for axis, dim in sides:
        size, length = (lax.axis_size(axis), array.shape[dim])
        up = [(i, (i + 1) % size) for i in range(size - 1)]
        down = [(j, i) for i, j in up]
        last = lax.slice_in_dim(array, length - width, length, axis=dim)
        first = lax.slice_in_dim(array, 0, width, axis=dim)
        before = lax.ppermute(last, axis, up)
        after = lax.ppermute(first, axis, down)
        array = jnp.concatenate([before, array, after], axis=dim)
    return array


def combined_all(array, axis, join):
    gathered = jax.tree.map(
        lambda a, kind: lax.all_gather(a.astype(kind), axis),
        array,
        (jnp.bfloat16, jnp.bfloat16, jnp.bfloat16),
    )

    def take(source):
        return jax.tree.map(
            lambda a, own: lax.dynamic_index_in_dim(a, source, 0, False).astype(own.dtype),
            gathered,
            array,
        )

    return lax.fori_loop(
        1, lax.axis_size(axis), lambda source, state: join(state, take(source)), take(0)
    )


def norm_rows(matrix_rows, norm_gain, norm_shift):
    center = matrix_rows - jnp.mean(matrix_rows, axis=-1, keepdims=True)
    spread = jnp.mean(center * center, axis=-1, keepdims=True)
    return center * lax.rsqrt(spread + epsilon) * norm_gain + norm_shift


def gelu_tanh(inputs):
    return jax.nn.gelu(inputs, approximate=True)


def softmax_with_mask(score_matrix, allowed, reduce_axis):
    row_top = jnp.max(jnp.where(allowed, score_matrix, -1e30), axis=reduce_axis, keepdims=True)
    raised = jnp.where(allowed, jnp.exp(jnp.where(allowed, score_matrix - row_top, 0.0)), 0.0)
    return raised / jnp.sum(raised, axis=reduce_axis, keepdims=True)


def newton_schulz_inverse(matrix):
    identity = jnp.eye(matrix.shape[-1], dtype=matrix.dtype)
    frobenius = jnp.sum(matrix * matrix, axis=(1, 2), keepdims=True)
    approx = jnp.swapaxes(matrix, 1, 2) / frobenius
    for sweep_index in range(NEWTON):
        product = jnp.einsum("hij,hjk->hik", matrix, approx, precision=highest_precision)
        factor = 7.0 * identity - product
        factor = 15.0 * identity - jnp.einsum(
            "hij,hjk->hik", product, factor, precision=highest_precision
        )
        factor = 13.0 * identity - jnp.einsum(
            "hij,hjk->hik", product, factor, precision=highest_precision
        )
        approx = 0.25 * jnp.einsum("hij,hjk->hik", approx, factor, precision=highest_precision)
    return approx


def land_inverse(landmark_query_rows, landmark_key_rows, allowed, scores_scale_factor):
    score_matrix = (
        jnp.einsum(
            "cri,fri->rcf", landmark_query_rows, landmark_key_rows, precision=highest_precision
        )
        * scores_scale_factor
    )
    return newton_schulz_inverse(softmax_with_mask(score_matrix, allowed, 2))


def fold_parts(first_part, second_part):
    top_first, total_first, acc_first = first_part
    top_second, total_second, acc_second = second_part
    joined = jnp.maximum(top_first, top_second)
    weight_first = jnp.exp(top_first - joined)
    weight_second = jnp.exp(top_second - joined)
    return (
        joined,
        total_first * weight_first + total_second * weight_second,
        acc_first * weight_first[:, :, None] + acc_second * weight_second[:, :, None],
    )


def local(
    x_in,
    out_cot,
    seg_ids,
    land_doc,
    w_qkv,
    w_out,
    w_up,
    w_down,
    conv_taps,
    head_bias,
    ffn_bias,
    gains,
    offsets,
):
    seg_all, doc_all = (
        lax.all_gather(seg_ids, "ctx", axis=1, tiled=True),
        lax.all_gather(land_doc, "ctx", axis=1, tiled=True),
    )
    ctx_place = lax.axis_index("ctx")
    tok_count = x_in.shape[1]
    model_width = x_in.shape[2]
    land_local = land_doc.shape[1]
    land_count = doc_all.shape[1]
    seg_len = tok_count // land_local
    local_width = w_qkv.shape[2]
    ffn_local = w_up.shape[1]
    head_count = local_width // HEAD_DIM
    conv_reach = KW // 2
    scores_scale_factor = HEAD_DIM ** (-0.5)
    tap_cols = jnp.repeat(conv_taps, HEAD_DIM, axis=1)
    fetch_weights = lambda: (
        lax.all_gather(w_qkv, ("fsdp", "ctx"), axis=0, tiled=True),
        lax.all_gather(w_out, ("fsdp", "ctx"), axis=0, tiled=True),
        lax.all_gather(w_up, ("fsdp", "ctx"), axis=0, tiled=True),
        lax.all_gather(w_down, ("fsdp", "ctx"), axis=0, tiled=True),
    )

    def add_rims(block_rows):
        return with_halo(block_rows, (("ctx", 0),), conv_reach)

    def head_sum(partial_value):
        return lax.psum(partial_value.astype(jnp.bfloat16), "tp").astype(jnp.float32)

    def land_mean(rows_low):
        return jnp.mean(
            rows_low.astype(jnp.float32).reshape(land_local, seg_len, local_width), axis=1
        ).astype(jnp.bfloat16)

    def heads_of(matrix):
        return matrix.reshape(matrix.shape[0], head_count, HEAD_DIM)

    def micro_step(totals_carry, micro_batch):
        tokens_low, cot_low, seg_full, doc_full = micro_batch
        qkv_full, out_full, up_full, down_full = fetch_weights()
        seg_local = lax.dynamic_slice_in_dim(seg_full, ctx_place * tok_count, tok_count)
        seg_pad = lax.dynamic_slice_in_dim(
            jnp.pad(seg_full, conv_reach, constant_values=-1),
            ctx_place * tok_count,
            tok_count + 2 * conv_reach,
        )
        token_mask = (doc_full[:, None] == seg_local[None, :])[None]
        landmark_mask = (doc_full[:, None] == doc_full[None, :])[None]
        projected = jnp.einsum(
            "td,dce->tce", tokens_low, qkv_full, preferred_element_type=jnp.float32
        )
        queries = (projected[:, 0] + head_bias[0]).astype(jnp.bfloat16)
        key_rows = projected[:, 1].astype(jnp.bfloat16)
        values = (projected[:, 2] + head_bias[1]).astype(jnp.bfloat16)
        land_query, land_key = (
            lax.all_gather(land_mean(queries), "ctx", axis=0, tiled=True),
            lax.all_gather(land_mean(key_rows), "ctx", axis=0, tiled=True),
        )
        heads_of_queries = heads_of(queries)
        heads_of_keys = heads_of(key_rows)
        heads_of_values = heads_of(values)
        landmark_queries = heads_of(land_query)
        landmark_keys = heads_of(land_key)
        scores_tok = (
            jnp.einsum(
                "xpf,gpf->pxg", landmark_keys, heads_of_queries, preferred_element_type=jnp.float32
            )
            * scores_scale_factor
        )
        token_kernel = softmax_with_mask(scores_tok, token_mask, 1)

        def inverse_of(query_part, key_part):
            return land_inverse(query_part, key_part, landmark_mask, scores_scale_factor)

        mixer_matrix, mixer_pull = jax.vjp(
            inverse_of, landmark_queries.astype(jnp.float32), landmark_keys.astype(jnp.float32)
        )
        scores_key = (
            jnp.einsum(
                "xpf,gpf->pxg", landmark_queries, heads_of_keys, preferred_element_type=jnp.float32
            )
            * scores_scale_factor
        )
        part_top = jnp.max(jnp.where(token_mask, scores_key, -1e30), axis=2)
        partial_exponent = jnp.where(
            token_mask, jnp.exp(jnp.where(token_mask, scores_key - part_top[:, :, None], 0.0)), 0.0
        )
        value_as_float = heads_of_values.astype(jnp.float32)
        partial_accumulator = jnp.einsum(
            "iaf,fig->iag", partial_exponent, value_as_float, precision=highest_precision
        )
        row_top, row_total, row_acc = combined_all(
            (part_top, jnp.sum(partial_exponent, axis=2), partial_accumulator), "ctx", fold_parts
        )
        landmark_values = row_acc / row_total[:, :, None]
        mixing_weights = jnp.einsum(
            "ugy,uyx->ugx", mixer_matrix, landmark_values, precision=highest_precision
        )
        attended_output = jnp.einsum(
            "qsf,qsg->fqg", token_kernel, mixing_weights, precision=highest_precision
        )
        value_pad = add_rims(values)
        conv_sum = jnp.zeros((tok_count, local_width), jnp.float32)
        for tap_index in range(KW):
            same_doc = (seg_pad[tap_index : tap_index + tok_count] == seg_local)[:, None]
            window = value_pad[tap_index : tap_index + tok_count].astype(jnp.float32)
            conv_sum = conv_sum + jnp.where(same_doc, tap_cols[tap_index] * window, 0.0)
        mixed_rows = (attended_output.reshape(tok_count, local_width) + conv_sum).astype(
            jnp.bfloat16
        )
        branch = (
            head_sum(
                jnp.einsum("te,de->td", mixed_rows, out_full, preferred_element_type=jnp.float32)
            )
            + offsets[2]
        )
        hidden, pull_first = jax.vjp(
            norm_rows, tokens_low.astype(jnp.float32) + branch, gains[0], offsets[0]
        )
        hidden_low = hidden.astype(jnp.bfloat16)
        upward = (
            jnp.einsum("td,df->tf", hidden_low, up_full, preferred_element_type=jnp.float32)
            + ffn_bias
        )
        active, gelu_pull = jax.vjp(gelu_tanh, upward)
        active_low = active.astype(jnp.bfloat16)
        ffn_out = (
            head_sum(
                jnp.einsum("tf,df->td", active_low, down_full, preferred_element_type=jnp.float32)
            )
            + offsets[3]
        )
        output, pull_second = jax.vjp(norm_rows, hidden + ffn_out, gains[1], offsets[1])
        qkv_back, out_back, up_back, down_back = fetch_weights()
        grad_second, gain_second, shift_second = pull_second(cot_low.astype(jnp.float32))
        grad_ffn = grad_second.astype(jnp.bfloat16)
        down_grad = jnp.einsum(
            "td,tf->df", grad_ffn, active_low, preferred_element_type=jnp.float32
        )
        grad_active = jnp.einsum(
            "td,df->tf", grad_ffn, down_back, preferred_element_type=jnp.float32
        )
        grad_upward = gelu_pull(grad_active)[0].astype(jnp.bfloat16)
        up_grad = jnp.einsum(
            "td,tf->df", hidden_low, grad_upward, preferred_element_type=jnp.float32
        )
        grad_hidden = (
            head_sum(
                jnp.einsum("tf,df->td", grad_upward, up_back, preferred_element_type=jnp.float32)
            )
            + grad_second
        )
        grad_first, gain_first, shift_first = pull_first(grad_hidden)
        grad_branch = grad_first.astype(jnp.bfloat16)
        out_grad = jnp.einsum(
            "td,te->de", grad_branch, mixed_rows, preferred_element_type=jnp.float32
        )
        grad_mixed = jnp.einsum(
            "td,de->te", grad_branch, out_back, preferred_element_type=jnp.float32
        ).astype(jnp.bfloat16)
        heads_gradient = heads_of(grad_mixed).astype(jnp.float32)
        token_kernel_gradient = jnp.einsum(
            "pvl,bpl->pvb", mixing_weights, heads_gradient, precision=highest_precision
        )
        mixing_weights_gradient = lax.psum(
            jnp.einsum(
                "iaf,fig->iag", token_kernel, heads_gradient, precision=highest_precision
            ).astype(jnp.bfloat16),
            "ctx",
        ).astype(jnp.float32)
        grad_pad = add_rims(grad_mixed)
        grad_float = grad_mixed.astype(jnp.float32)
        value_grad = jnp.zeros((tok_count, local_width), jnp.float32)
        tap_rows = []
        for tap_index in range(KW):
            same_doc = (seg_pad[tap_index : tap_index + tok_count] == seg_local)[:, None]
            window = value_pad[tap_index : tap_index + tok_count].astype(jnp.float32)
            tap_rows.append(jnp.sum(jnp.where(same_doc, grad_float * window, 0.0), axis=0))
            mirror = 2 * conv_reach - tap_index
            same_back = (seg_pad[mirror : mirror + tok_count] == seg_local)[:, None]
            value_grad = value_grad + jnp.where(
                same_back,
                tap_cols[tap_index] * grad_pad[mirror : mirror + tok_count].astype(jnp.float32),
                0.0,
            )
        tap_grad = jnp.sum(jnp.stack(tap_rows).reshape(KW, head_count, HEAD_DIM), axis=2)
        landmark_values_gradient = jnp.einsum(
            "xvs,xvb->xsb", mixer_matrix, mixing_weights_gradient, precision=highest_precision
        )
        mixer_matrix_gradient = jnp.einsum(
            "fbi,fpi->fbp", mixing_weights_gradient, landmark_values, precision=highest_precision
        )
        land_query_mix, land_key_mix = mixer_pull(mixer_matrix_gradient)
        keys_kernel_matrix = (
            jnp.where(
                token_mask,
                jnp.exp(jnp.where(token_mask, scores_key - row_top[:, :, None], 0.0)),
                0.0,
            )
            / row_total[:, :, None]
        )
        grad_kernel_keys = jnp.einsum(
            "pvl,bpl->pvb", landmark_values_gradient, value_as_float, precision=highest_precision
        )
        center_keys = jnp.sum(landmark_values_gradient * landmark_values, axis=2)
        key_scores_gradient = (
            keys_kernel_matrix * (grad_kernel_keys - center_keys[:, :, None]) * scores_scale_factor
        )
        value_grad = value_grad + jnp.einsum(
            "qsf,qsg->fqg",
            keys_kernel_matrix,
            landmark_values_gradient,
            precision=highest_precision,
        ).reshape(tok_count, local_width)
        land_query_part = jnp.einsum(
            "uke,euo->kuo",
            key_scores_gradient,
            heads_of_keys.astype(jnp.float32),
            precision=highest_precision,
        )
        key_grad = jnp.einsum(
            "que,uqb->eqb",
            key_scores_gradient,
            landmark_queries.astype(jnp.float32),
            precision=highest_precision,
        )
        center_tok = jnp.sum(token_kernel * token_kernel_gradient, axis=1, keepdims=True)
        token_scores_gradient = (
            token_kernel * (token_kernel_gradient - center_tok) * scores_scale_factor
        )
        query_grad = jnp.einsum(
            "que,uqb->eqb",
            token_scores_gradient,
            landmark_keys.astype(jnp.float32),
            precision=highest_precision,
        )
        land_key_part = jnp.einsum(
            "uke,euo->kuo",
            token_scores_gradient,
            heads_of_queries.astype(jnp.float32),
            precision=highest_precision,
        )
        own_query, own_key = (
            lax.psum_scatter(
                land_query_part.reshape(land_count, local_width).astype(jnp.bfloat16),
                "ctx",
                scatter_dimension=0,
                tiled=True,
            ).astype(jnp.float32),
            lax.psum_scatter(
                land_key_part.reshape(land_count, local_width).astype(jnp.bfloat16),
                "ctx",
                scatter_dimension=0,
                tiled=True,
            ).astype(jnp.float32),
        )
        own_query = own_query + lax.dynamic_slice_in_dim(
            land_query_mix.reshape(land_count, local_width), ctx_place * land_local, land_local
        )
        own_key = own_key + lax.dynamic_slice_in_dim(
            land_key_mix.reshape(land_count, local_width), ctx_place * land_local, land_local
        )
        grad_queries = (
            query_grad.reshape(tok_count, local_width)
            + jnp.repeat(own_query / seg_len, seg_len, axis=0)
        ).astype(jnp.bfloat16)
        grad_keys = (
            key_grad.reshape(tok_count, local_width)
            + jnp.repeat(own_key / seg_len, seg_len, axis=0)
        ).astype(jnp.bfloat16)
        grad_values = value_grad.astype(jnp.bfloat16)
        grad_proj = jnp.stack([grad_queries, grad_keys, grad_values], axis=1)
        qkv_grad = jnp.einsum(
            "td,tce->dce", tokens_low, grad_proj, preferred_element_type=jnp.float32
        )
        grad_tokens = (
            head_sum(
                jnp.einsum("tce,dce->td", grad_proj, qkv_back, preferred_element_type=jnp.float32)
            )
            + grad_first
        )
        bias_grad = jnp.stack(
            [
                jnp.sum(grad_queries.astype(jnp.float32), axis=0),
                jnp.sum(grad_values.astype(jnp.float32), axis=0),
            ]
        )
        ffn_bias_grad = jnp.sum(grad_upward.astype(jnp.float32), axis=0)
        gain_grad = jnp.stack([gain_first, gain_second])
        offset_grad = jnp.stack(
            [
                shift_first,
                shift_second,
                jnp.sum(grad_branch.astype(jnp.float32), axis=0),
                jnp.sum(grad_ffn.astype(jnp.float32), axis=0),
            ]
        )
        weight_grads = (qkv_grad, out_grad, up_grad, down_grad)
        small_grads = (tap_grad, bias_grad, ffn_bias_grad, gain_grad, offset_grad)
        new_carry = jax.tree.map(
            lambda earlier, update: earlier + update, totals_carry, (weight_grads, small_grads)
        )
        return (new_carry, (output.astype(jnp.bfloat16), grad_tokens.astype(jnp.bfloat16)))

    big_start = (
        jnp.zeros((model_width, 3, local_width), jnp.float32),
        jnp.zeros((model_width, local_width), jnp.float32),
        jnp.zeros((model_width, ffn_local), jnp.float32),
        jnp.zeros((model_width, ffn_local), jnp.float32),
    )
    small_start = (
        jnp.zeros((KW, head_count), jnp.float32),
        jnp.zeros((2, local_width), jnp.float32),
        jnp.zeros((ffn_local,), jnp.float32),
        jnp.zeros((2, model_width), jnp.float32),
        jnp.zeros((4, model_width), jnp.float32),
    )
    (big_total, small_total), (outputs, input_grads) = lax.scan(
        micro_step, (big_start, small_start), (x_in, out_cot, seg_all, doc_all)
    )
    weight_shards = (
        lax.psum_scatter(big_total[0], ("fsdp", "ctx"), scatter_dimension=0, tiled=True),
        lax.psum_scatter(big_total[1], ("fsdp", "ctx"), scatter_dimension=0, tiled=True),
        lax.psum_scatter(big_total[2], ("fsdp", "ctx"), scatter_dimension=0, tiled=True),
        lax.psum_scatter(big_total[3], ("fsdp", "ctx"), scatter_dimension=0, tiled=True),
    )
    small_sums = lax.psum(
        (small_total[0], small_total[1], small_total[2], small_total[3], small_total[4]),
        ("fsdp", "ctx"),
    )
    return (
        outputs,
        input_grads,
        weight_shards[0],
        weight_shards[1],
        weight_shards[2],
        weight_shards[3],
        small_sums[0],
        small_sums[1],
        small_sums[2],
        small_sums[3],
        small_sums[4],
    )


def solution(mesh):
    placed = (
        P("fsdp", "ctx", None),
        P("fsdp", "ctx", None),
        P("fsdp", "ctx"),
        P("fsdp", "ctx"),
        P(("fsdp", "ctx"), None, "tp"),
        P(("fsdp", "ctx"), "tp"),
        P(("fsdp", "ctx"), "tp"),
        P(("fsdp", "ctx"), "tp"),
        P(None, "tp"),
        P(None, "tp"),
        P("tp"),
        P(),
        P(),
    )
    return jax.shard_map(
        local,
        mesh=mesh,
        in_specs=placed,
        out_specs=(
            P("fsdp", "ctx", None),
            P("fsdp", "ctx", None),
            P(("fsdp", "ctx"), None, "tp"),
            P(("fsdp", "ctx"), "tp"),
            P(("fsdp", "ctx"), "tp"),
            P(("fsdp", "ctx"), "tp"),
            P(None, "tp"),
            P(None, "tp"),
            P("tp"),
            P(),
            P(),
        ),
        check_vma=False,
    )
```

profile of v0, /device:TPU:0, one launch (start us, length us, event | category | flops | bytes accessed | tf_op | source)
XLA Modules:
  0.0 1283.5 jit_solution(10366434358086685104)
XLA Ops:
  34.0 949.4 %while.81 = (s32[]{:T(128)}, f32[768,3,384]{2,0,1:T(8,128)}, f32[768,384]{1,0:T(8,128)}, f32[768,1536]{1,0:T(8,128)}, f32[768,1536]{1,0:T(8,128)}, /*index=5*/f3...) while((s32[]{:T(128)}, f32[768,3,384]{2,0,1:T(8,128)}, ...), condition=%wide.region_76.77_spmd.clone, body=%wide.region_0.76_spmd.clone.sunk | while | flops 7800943616 | bytes 263048928 | solution.py:435
  39.4 37.6 %all_gather.119 = bf16[768,384]{1,0:T(8,128)(2,1)S(1)} all-gather(bf16[48,384]{1,0:T(8,128)(2,1)} %get-tuple-element.1858), channel_id=1, replica_groups=mesh['fsdp'=4,'ctx'=4,'tp'=2] {'fsdp','ctx'}, dimensions={0}, use_global_device_ids=true | all-gather | bytes 626688 | tf_op jit(solution)/shard_map/while/body/eval_jaxpr/all_gather | solution.py:136
  151.6 14.2 %all-gather.14 = bf16[24,64,64]{2,1,0:T(8,128)(2,1)S(1)} all-gather(bf16[6,64,64]{2,1,0:T(8,128)(2,1)S(1)} %convolution_convert_fusion.15), channel_id=4, replica_groups=mesh['fsdp'=4,'ctx'=4,'tp'=2] {'ctx'}, dimensions={0}, use_global_device_ids=true | all-gather | bytes 245760 | tf_op jit(solution)/shard_map/while/body/eval_jaxpr/all_gather | solution.py:30
  181.0 20.4 %all-reduce.7.cloned.1.call-done = bf16[256,768]{1,0:T(8,128)(2,1)} async-done(((bf16[256,768]{1,0:T(8,128)(2,1)}), bf16[256,768]{1,0:T(8,128)(2,1)}) %all-reduce.7.cloned.1.call-update) | async-done | bytes 393232 | tf_op jit(solution)/shard_map/while/body/eval_jaxpr/psum | solution.py:145
  204.0 42.3 %all-gather.23.cloned.1.call-done = bf16[768,1536]{1,0:T(8,128)(2,1)} async-done(((bf16[48,1536]{1,0:T(8,128)(2,1)}), bf16[768,1536]{1,0:T(8,128)(2,1)}) %all-gather.23.cloned.1.call-update) | async-done | bytes 2359312 | tf_op jit(solution)/shard_map/while/body/eval_jaxpr/all_gather | solution.py:137
  250.0 39.7 %all-gather.21.cloned.1.call-done = bf16[768,1536]{1,0:T(8,128)(2,1)} async-done(((bf16[48,1536]{1,0:T(8,128)(2,1)}), bf16[768,1536]{1,0:T(8,128)(2,1)}) %all-gather.21.cloned.1.call-update) | async-done | bytes 2359312 | tf_op jit(solution)/shard_map/while/body/eval_jaxpr/all_gather | solution.py:138
  295.0 23.4 %all-reduce.9.cloned.1.call-done = bf16[256,768]{1,0:T(8,128)(2,1)} async-done(((bf16[256,768]{1,0:T(8,128)(2,1)}), bf16[256,768]{1,0:T(8,128)(2,1)}) %all-reduce.9.cloned.1.call-update) | async-done | bytes 393232 | tf_op jit(solution)/shard_map/while/body/eval_jaxpr/psum | solution.py:145
  338.3 15.6 %all-reduce.11.cloned.1.call-done = bf16[256,768]{1,0:T(8,128)(2,1)} async-done(((bf16[256,768]{1,0:T(8,128)(2,1)}), bf16[256,768]{1,0:T(8,128)(2,1)}) %all-reduce.11.cloned.1.call-update) | async-done | bytes 393232 | tf_op jit(solution)/shard_map/while/body/eval_jaxpr/psum | solution.py:145
  363.0 21.1 %psum.118 = bf16[6,64,64]{2,1,0:T(8,128)(2,1)S(1)} all-reduce(bf16[6,64,64]{2,1,0:T(8,128)(2,1)} %convolution_convert_fusion.19), channel_id=1, replica_groups=mesh['fsdp'=4,'ctx'=4,'tp'=2] {'ctx'}, use_global_device_ids=true, to_apply=%region_24.24 | all-reduce | flops 24576 | bytes 98304 | tf_op jit(solution)/shard_map/while/body/eval_jaxpr/psum | solution.py:282
  463.4 13.5 %reduce-scatter.15.cloned.1.call-done = bf16[16,384]{1,0:T(8,128)(2,1)} async-done(((bf16[64,384]{1,0:T(8,128)(2,1)}), bf16[16,384]{1,0:T(8,128)(2,1)}) %reduce-scatter.15.cloned.1.call-update) | async-done | bytes 12304 | tf_op jit(solution)/shard_map/while/body/eval_jaxpr/reduce_scatter | solution.py:367
  483.4 21.4 %all-reduce.13.cloned.1.call-done = bf16[256,768]{1,0:T(8,128)(2,1)} async-done(((bf16[256,768]{1,0:T(8,128)(2,1)}), bf16[256,768]{1,0:T(8,128)(2,1)}) %all-reduce.13.cloned.1.call-update) | async-done | bytes 393232 | tf_op jit(solution)/shard_map/while/body/eval_jaxpr/psum | solution.py:145
  511.9 40.7 %all_gather.119 = bf16[768,384]{1,0:T(8,128)(2,1)S(1)} all-gather(bf16[48,384]{1,0:T(8,128)(2,1)} %get-tuple-element.1858), channel_id=1, replica_groups=mesh['fsdp'=4,'ctx'=4,'tp'=2] {'fsdp','ctx'}, dimensions={0}, use_global_device_ids=true | all-gather | bytes 626688 | tf_op jit(solution)/shard_map/while/body/eval_jaxpr/all_gather | solution.py:136
  560.1 13.7 %all_gather.118 = bf16[64,384]{1,0:T(8,128)(2,1)S(1)} all-gather(bf16[16,384]{1,0:T(8,128)(2,1)S(1)} %multiply_convert_fusion.12), channel_id=1, replica_groups=mesh['fsdp'=4,'ctx'=4,'tp'=2] {'ctx'}, dimensions={0}, use_global_device_ids=true | all-gather | bytes 61440 | tf_op jit(solution)/shard_map/while/body/eval_jaxpr/all_gather | solution.py:174
  625.8 14.2 %all-gather.14 = bf16[24,64,64]{2,1,0:T(8,128)(2,1)S(1)} all-gather(bf16[6,64,64]{2,1,0:T(8,128)(2,1)S(1)} %convolution_convert_fusion.15), channel_id=4, replica_groups=mesh['fsdp'=4,'ctx'=4,'tp'=2] {'ctx'}, dimensions={0}, use_global_device_ids=true | all-gather | bytes 245760 | tf_op jit(solution)/shard_map/while/body/eval_jaxpr/all_gather | solution.py:30
  655.2 21.4 %all-reduce.7.cloned.1.call-done = bf16[256,768]{1,0:T(8,128)(2,1)} async-done(((bf16[256,768]{1,0:T(8,128)(2,1)}), bf16[256,768]{1,0:T(8,128)(2,1)}) %all-reduce.7.cloned.1.call-update) | async-done | bytes 393232 | tf_op jit(solution)/shard_map/while/body/eval_jaxpr/psum | solution.py:145
  679.2 42.1 %all-gather.23.cloned.1.call-done = bf16[768,1536]{1,0:T(8,128)(2,1)} async-done(((bf16[48,1536]{1,0:T(8,128)(2,1)}), bf16[768,1536]{1,0:T(8,128)(2,1)}) %all-gather.23.cloned.1.call-update) | async-done | bytes 2359312 | tf_op jit(solution)/shard_map/while/body/eval_jaxpr/all_gather | solution.py:137
  725.1 39.9 %all-gather.21.cloned.1.call-done = bf16[768,1536]{1,0:T(8,128)(2,1)} async-done(((bf16[48,1536]{1,0:T(8,128)(2,1)}), bf16[768,1536]{1,0:T(8,128)(2,1)}) %all-gather.21.cloned.1.call-update) | async-done | bytes 2359312 | tf_op jit(solution)/shard_map/while/body/eval_jaxpr/all_gather | solution.py:138
  770.3 23.4 %all-reduce.9.cloned.1.call-done = bf16[256,768]{1,0:T(8,128)(2,1)} async-done(((bf16[256,768]{1,0:T(8,128)(2,1)}), bf16[256,768]{1,0:T(8,128)(2,1)}) %all-reduce.9.cloned.1.call-update) | async-done | bytes 393232 | tf_op jit(solution)/shard_map/while/body/eval_jaxpr/psum | solution.py:145
  838.2 21.1 %psum.118 = bf16[6,64,64]{2,1,0:T(8,128)(2,1)S(1)} all-reduce(bf16[6,64,64]{2,1,0:T(8,128)(2,1)} %convolution_convert_fusion.19), channel_id=1, replica_groups=mesh['fsdp'=4,'ctx'=4,'tp'=2] {'ctx'}, use_global_device_ids=true, to_apply=%region_24.24 | all-reduce | flops 24576 | bytes 98304 | tf_op jit(solution)/shard_map/while/body/eval_jaxpr/psum | solution.py:282
  960.5 19.3 %all-reduce.13.cloned.1.call-done = bf16[256,768]{1,0:T(8,128)(2,1)} async-done(((bf16[256,768]{1,0:T(8,128)(2,1)}), bf16[256,768]{1,0:T(8,128)(2,1)}) %all-reduce.13.cloned.1.call-update) | async-done | bytes 393232 | tf_op jit(solution)/shard_map/while/body/eval_jaxpr/psum | solution.py:145
  986.1 62.4 %all-reduce.1 = (f32[33,6]{0,1:T(8,128)}, f32[2,384]{1,0:T(2,128)}, f32[1536]{0:T(1024)}, f32[2,768]{1,0:T(2,128)}, f32[4,768]{1,0:T(4,128)}) all-reduce(f32[33,6]{0,1:T(8,128)S(1)} %copy.192, f32[2,384]{1,0:T(2,128)S(1)} %copy-done.231, f32[1536]{0:T(1024)} %get-tuple-element.850, ...), channel_id=1, replica_groups=mesh['fsdp'=4,'ctx'=4,'tp'=2] {'fsdp','ctx'}, use_global_device_ids=true, to_apply=%region_81.82 | all-reduce | flops 7110 | bytes 56880 | tf_op jit(solution)/shard_map/psum | solution.py:444
  1048.5 69.0 %reduce-scatter.7.cloned.1.call-done = f32[48,3,384]{2,0,1:T(8,128)} async-done(((f32[768,3,384]{2,0,1:T(8,128)}), f32[48,3,384]{2,0,1:T(8,128)}) %reduce-scatter.7.cloned.1.call-update) | async-done | bytes 221200 | tf_op jit(solution)/shard_map/reduce_scatter | solution.py:439
  1117.4 78.7 %reduce-scatter.11.cloned.1.call-done = f32[48,1536]{1,0:T(8,128)} async-done(((f32[768,1536]{1,0:T(8,128)}), f32[48,1536]{1,0:T(8,128)}) %reduce-scatter.11.cloned.1.call-update) | async-done | bytes 294928 | tf_op jit(solution)/shard_map/reduce_scatter | solution.py:441
  1196.2 79.5 %reduce-scatter.13.cloned.1.call-done = f32[48,1536]{1,0:T(8,128)} async-done(((f32[768,1536]{1,0:T(8,128)}), f32[48,1536]{1,0:T(8,128)}) %reduce-scatter.13.cloned.1.call-update) | async-done | bytes 294928 | tf_op jit(solution)/shard_map/reduce_scatter | solution.py:442
  (1667 shorter events, 483.2 us)
Async XLA Ops:
  34.3 43.6 %all-gather.19.cloned.1.call-start = ((), (), s32[]{:S(2)}) async-start(), calls=%async_computation.10 | async-start | bytes 1880064 | tf_op jit(solution)/shard_map/while/body/eval_jaxpr/all_gather | solution.py:135
  35.0 166.3 %all-reduce.7.cloned.1.call-start = ((), (), s32[]{:S(2)}) async-start(), calls=%async_computation.11 | async-start | bytes 786432 | tf_op jit(solution)/shard_map/while/body/eval_jaxpr/psum | solution.py:145
  81.0 87.6 %collective-permute-start = (bf16[16,384]{1,0:T(8,128)(2,1)}, bf16[16,384]{1,0:T(8,128)(2,1)}, u32[]{:S(2)}, u32[]{:S(2)}) collective-permute-start(bf16[16,384]{1,0:T(8,128)(2,1)} %get-tuple-element.1582), channel_id=1, source_target_pairs={{0,2},{2,4},{4,6},{1,3},{3,5},{5,7},{8,10},{10,12},{12,14},{9,11},... | collective-permute-start | bytes 36872 | tf_op jit(solution)/shard_map/while/body/eval_jaxpr/ppermute | solution.py:22
  84.4 84.2 %collective-permute-start.1 = (bf16[16,384]{1,0:T(8,128)(2,1)}, bf16[16,384]{1,0:T(8,128)(2,1)}, u32[]{:S(2)}, u32[]{:S(2)}) collective-permute-start(bf16[16,384]{1,0:T(8,128)(2,1)} %get-tuple-element.1588), channel_id=1, source_target_pairs={{2,0},{4,2},{6,4},{3,1},{5,3},{7,5},{10,8},{12,10},{14,12},{11,9},... | collective-permute-start | bytes 36872 | tf_op jit(solution)/shard_map/while/body/eval_jaxpr/ppermute | solution.py:23
  177.5 68.7 %all-gather.23.cloned.1.call-start = ((), (), s32[]{:S(2)}) async-start(), calls=%async_computation.13 | async-start | bytes 2506752 | tf_op jit(solution)/shard_map/while/body/eval_jaxpr/all_gather | solution.py:137
  178.3 111.5 %all-gather.21.cloned.1.call-start = ((), (), s32[]{:S(2)}) async-start(), calls=%async_computation.12 | async-start | bytes 2506752 | tf_op jit(solution)/shard_map/while/body/eval_jaxpr/all_gather | solution.py:138
  178.8 139.6 %all-reduce.9.cloned.1.call-start = ((), (), s32[]{:S(2)}) async-start(), calls=%async_computation.14 | async-start | bytes 786432 | tf_op jit(solution)/shard_map/while/body/eval_jaxpr/psum | solution.py:145
  293.8 60.2 %all-reduce.11.cloned.1.call-start = ((), (), s32[]{:S(2)}) async-start(), calls=%async_computation.15 | async-start | bytes 786432 | tf_op jit(solution)/shard_map/while/body/eval_jaxpr/psum | solution.py:145
  328.0 128.9 %reduce-scatter.17.cloned.1.call-start = ((), (), s32[]{:S(2)}) async-start(), calls=%async_computation.17 | async-start | bytes 61440 | tf_op jit(solution)/shard_map/while/body/eval_jaxpr/reduce_scatter | solution.py:361
  447.8 57.0 %all-reduce.13.cloned.1.call-start = ((), (), s32[]{:S(2)}) async-start(), calls=%async_computation.18 | async-start | bytes 786432 | tf_op jit(solution)/shard_map/while/body/eval_jaxpr/psum | solution.py:145
  507.0 45.6 %all-gather.19.cloned.1.call-start = ((), (), s32[]{:S(2)}) async-start(), calls=%async_computation.10 | async-start | bytes 1880064 | tf_op jit(solution)/shard_map/while/body/eval_jaxpr/all_gather | solution.py:135
  507.6 169.0 %all-reduce.7.cloned.1.call-start = ((), (), s32[]{:S(2)}) async-start(), calls=%async_computation.11 | async-start | bytes 786432 | tf_op jit(solution)/shard_map/while/body/eval_jaxpr/psum | solution.py:145
  555.9 86.9 %collective-permute-start = (bf16[16,384]{1,0:T(8,128)(2,1)}, bf16[16,384]{1,0:T(8,128)(2,1)}, u32[]{:S(2)}, u32[]{:S(2)}) collective-permute-start(bf16[16,384]{1,0:T(8,128)(2,1)} %get-tuple-element.1582), channel_id=1, source_target_pairs={{0,2},{2,4},{4,6},{1,3},{3,5},{5,7},{8,10},{10,12},{12,14},{9,11},... | collective-permute-start | bytes 36872 | tf_op jit(solution)/shard_map/while/body/eval_jaxpr/ppermute | solution.py:22
  558.1 84.6 %collective-permute-start.1 = (bf16[16,384]{1,0:T(8,128)(2,1)}, bf16[16,384]{1,0:T(8,128)(2,1)}, u32[]{:S(2)}, u32[]{:S(2)}) collective-permute-start(bf16[16,384]{1,0:T(8,128)(2,1)} %get-tuple-element.1588), channel_id=1, source_target_pairs={{2,0},{4,2},{6,4},{3,1},{5,3},{7,5},{10,8},{12,10},{14,12},{11,9},... | collective-permute-start | bytes 36872 | tf_op jit(solution)/shard_map/while/body/eval_jaxpr/ppermute | solution.py:23
  651.7 69.6 %all-gather.23.cloned.1.call-start = ((), (), s32[]{:S(2)}) async-start(), calls=%async_computation.13 | async-start | bytes 2506752 | tf_op jit(solution)/shard_map/while/body/eval_jaxpr/all_gather | solution.py:137
  652.3 112.7 %all-gather.21.cloned.1.call-start = ((), (), s32[]{:S(2)}) async-start(), calls=%async_computation.12 | async-start | bytes 2506752 | tf_op jit(solution)/shard_map/while/body/eval_jaxpr/all_gather | solution.py:138
  653.0 140.6 %all-reduce.9.cloned.1.call-start = ((), (), s32[]{:S(2)}) async-start(), calls=%async_computation.14 | async-start | bytes 786432 | tf_op jit(solution)/shard_map/while/body/eval_jaxpr/psum | solution.py:145
  769.0 60.2 %all-reduce.11.cloned.1.call-start = ((), (), s32[]{:S(2)}) async-start(), calls=%async_computation.15 | async-start | bytes 786432 | tf_op jit(solution)/shard_map/while/body/eval_jaxpr/psum | solution.py:145
  803.3 128.9 %reduce-scatter.17.cloned.1.call-start = ((), (), s32[]{:S(2)}) async-start(), calls=%async_computation.17 | async-start | bytes 61440 | tf_op jit(solution)/shard_map/while/body/eval_jaxpr/reduce_scatter | solution.py:361
  924.3 55.5 %all-reduce.13.cloned.1.call-start = ((), (), s32[]{:S(2)}) async-start(), calls=%async_computation.18 | async-start | bytes 786432 | tf_op jit(solution)/shard_map/while/body/eval_jaxpr/psum | solution.py:145
  983.5 65.0 %reduce-scatter.9.cloned.1.call-start = ((), (), s32[]{:S(2)}) async-start(), calls=%async_computation.7 | async-start | bytes 1253376 | tf_op jit(solution)/shard_map/reduce_scatter | solution.py:440
  984.1 133.4 %reduce-scatter.7.cloned.1.call-start = ((), (), s32[]{:S(2)}) async-start(), calls=%async_computation.6 | async-start | bytes 3760128 | tf_op jit(solution)/shard_map/reduce_scatter | solution.py:439
  984.7 211.5 %reduce-scatter.11.cloned.1.call-start = ((), (), s32[]{:S(2)}) async-start(), calls=%async_computation.8 | async-start | bytes 5013504 | tf_op jit(solution)/shard_map/reduce_scatter | solution.py:441
  985.2 290.4 %reduce-scatter.13.cloned.1.call-start = ((), (), s32[]{:S(2)}) async-start(), calls=%async_computation.9 | async-start | bytes 5013504 | tf_op jit(solution)/shard_map/reduce_scatter | solution.py:442
  (512 other events, 4842.7 us)
Sparse Core Ops, SparseCore 0:
  37.4 40.4 all-gather.18
  177.7 23.6 all-reduce.6
  204.0 42.2 all-gather.22
  248.7 41.0 all-gather.20
  293.9 24.5 all-reduce.8
  328.1 25.7 all-reduce.10
  438.0 18.8 reduce-scatter.16
  459.7 17.1 reduce-scatter.14
  480.9 23.8 all-reduce.12
  509.8 42.5 all-gather.18
  651.8 24.7 all-reduce.6
  679.1 42.2 all-gather.22
  723.9 41.0 all-gather.20
  769.1 24.5 all-reduce.8
  803.4 25.7 all-reduce.10
  913.2 18.8 reduce-scatter.16
  934.8 17.1 reduce-scatter.14
  955.9 23.8 all-reduce.12
Sparse Core Ops, SparseCore 1:
  988.1 58.0 reduce-scatter.8
  1050.6 66.8 reduce-scatter.6
  1121.8 74.4 reduce-scatter.10
  1201.1 74.5 reduce-scatter.12
where the time goes:
time: 1290 us; the launch traced here: 1280 us
  waiting for transfers between devices  584 us (45%)
  blocking collectives  338 us (26%)
  matrix products  168 us (13%)
  other arithmetic  84.8 us (7%)
  local copies, waits for them, and re-layouts  66.6 us (5%)
  between operations  16.1 us (1%)
  starting transfers between devices  15.5 us (1%)
    psum x8, waiting for transfers between devices, head_sum(): lax.psum(partial_value.astype(jnp.bfloat16), 'tp').astype(jnp.float32)  156 us
    all_gather x2, waiting for transfers between devices, local(): lax.all_gather(w_up, ('fsdp', 'ctx'), axis=0, tiled=True)  84.4 us
    all_gather x2, waiting for transfers between devices, local(): lax.all_gather(w_down, ('fsdp', 'ctx'), axis=0, tiled=True)  79.6 us
    reduce_scatter x1, waiting for transfers between devices, local(): lax.psum_scatter(big_total[3], ('fsdp', 'ctx'), scatter_dimension=0, tile...  79.5 us
    reduce_scatter x1, waiting for transfers between devices, local(): lax.psum_scatter(big_total[2], ('fsdp', 'ctx'), scatter_dimension=0, tile...  78.7 us
    all_gather x2, blocking collectives, local(): lax.all_gather(w_out, ('fsdp', 'ctx'), axis=0, tiled=True)  78.2 us
    all_gather x6, blocking collectives, combined_all(): lax.all_gather(a.astype(kind), axis)  77 us
    reduce_scatter x1, waiting for transfers between devices, local(): lax.psum_scatter(big_total[0], ('fsdp', 'ctx'), scatter_dimension=0, tile...  69 us
  transfers between devices with their start and end apart: 30, of which 20 were waited for; matrix products, arithmetic and copies ran while one was open for 11% of the time, Pallas kernels for 0%

commit v1 on v0

v1 whole, which is shorter than its diff:
```python
import jax
import jax.numpy as jnp
from jax import lax
from jax.experimental import pallas as pl
from jax.experimental.pallas import tpu as pltpu
from jax.sharding import PartitionSpec as P

HEAD_DIM = 64
KW = 33
REACH = KW // 2
NEWTON = 6
EPS = 1e-05
SCALE = HEAD_DIM**-0.5
BLOCK = 256
PACK = BLOCK // HEAD_DIM
BF = jnp.bfloat16
F32 = jnp.float32
HI = lax.Precision.HIGHEST


def dot(spec, a, b):
    return jnp.einsum(spec, a, b, preferred_element_type=F32)


def hdot(spec, a, b):
    return jnp.einsum(spec, a, b, preferred_element_type=F32, precision=HI)


def swap(a, axis, mask):
    return lax.ppermute(a, axis, [(i, i ^ mask) for i in range(lax.axis_size(axis))])


def grow(a, bit):
    return jnp.concatenate([a, swap(a, *bit)], axis=0)


def shrink(a, bit):
    half = a.shape[0] // 2
    got = swap(a[half:], *bit)
    return (a[:half].astype(F32) + got.astype(F32)).astype(a.dtype)


def nn(a, b):
    return lax.dot_general(a, b, (((1,), (0,)), ((), ())), preferred_element_type=F32)


def nt(a, b):
    return lax.dot_general(a, b, (((1,), (1,)), ((), ())), preferred_element_type=F32)


def tn(a, b):
    return lax.dot_general(a, b, (((0,), (0,)), ((), ())), preferred_element_type=F32)


def lane_head(rows):
    return lax.broadcasted_iota(jnp.int32, (rows, BLOCK), 1) // HEAD_DIM


def expand(r):
    head = lane_head(HEAD_DIM)
    wide = r.astype(F32)
    return jnp.concatenate([jnp.where(head == i, wide, 0.0) for i in range(PACK)], 0).astype(r.dtype)


def compress(full):
    head = lane_head(HEAD_DIM)
    out = jnp.zeros((HEAD_DIM, BLOCK), F32)
    for i in range(PACK):
        out = jnp.where(head == i, full[i * HEAD_DIM : (i + 1) * HEAD_DIM], out)
    return out


def split(a):
    high = a.astype(BF)
    return high, (a - high.astype(F32)).astype(BF)


def mm3(a, b):
    ah, al = split(a)
    bh, bl = split(b)
    wide = expand(bh)
    return nn(ah, wide) + nn(al, wide) + nn(ah, expand(bl))


def tn3(a, b):
    ah, al = split(a)
    bh, bl = split(b)
    return compress(tn(ah, bh) + tn(al, bh) + tn(ah, bl))


def eye_row():
    row = lax.broadcasted_iota(jnp.int32, (HEAD_DIM, BLOCK), 0)
    lane = lax.broadcasted_iota(jnp.int32, (HEAD_DIM, BLOCK), 1)
    return jnp.where(row == lane % HEAD_DIM, 1.0, 0.0)


def head_total(a):
    head = lane_head(1)
    col = jnp.sum(a, axis=0, keepdims=True)
    out = jnp.zeros_like(col)
    for i in range(PACK):
        one = jnp.sum(jnp.where(head == i, col, 0.0), axis=1, keepdims=True)
        out = jnp.where(head == i, one, out)
    return out


def heads_sum(a):
    parts = a.reshape(PACK, HEAD_DIM, a.shape[1])
    return jnp.broadcast_to(jnp.sum(parts, axis=1, keepdims=True), parts.shape).reshape(a.shape)


def heads_max(a):
    parts = a.reshape(PACK, HEAD_DIM, a.shape[1])
    return jnp.broadcast_to(jnp.max(parts, axis=1, keepdims=True), parts.shape).reshape(a.shape)


def tall(mask):
    return jnp.concatenate([mask] * PACK, 0) > 0.5


def group(g):
    return slice(g * BLOCK, (g + 1) * BLOCK)


def scores_body(q_ref, k_ref, v_ref, land_ref, mask_ref, ktok_ref, ekey_ref, pack_ref):
    E = q_ref.shape[1]
    allowed = tall(mask_ref[...])
    lane = lax.broadcasted_iota(jnp.int32, (HEAD_DIM, 128), 1)
    stats = jnp.zeros((HEAD_DIM, 128), F32)
    heads = E // HEAD_DIM
    for g in range(E // BLOCK):
        s = group(g)
        lq, lk = land_ref[:, s], land_ref[:, E + g * BLOCK : E + (g + 1) * BLOCK]
        z = nt(expand(lk), q_ref[:, s]) * SCALE
        z = jnp.where(allowed, z, -1e30)
        e = jnp.where(allowed, jnp.exp(z - heads_max(z)), 0.0)
        ktok_ref[s, :] = (e / heads_sum(e)).astype(BF)
        z = nt(expand(lq), k_ref[:, s]) * SCALE
        z = jnp.where(allowed, z, -1e30)
        top = jnp.max(z, axis=1, keepdims=True)
        e = jnp.where(allowed, jnp.exp(z - top), 0.0)
        total = jnp.sum(e, axis=1, keepdims=True)
        low = e.astype(BF)
        ekey_ref[s, :] = low
        pack_ref[:, s] = compress(nn(low, v_ref[:, s])).astype(BF)
        for i in range(PACK):
            h = g * PACK + i
            rows = slice(i * HEAD_DIM, (i + 1) * HEAD_DIM)
            stats = jnp.where(lane == h, top[rows], stats)
            stats = jnp.where(lane == heads + h, total[rows], stats)
    first = stats.astype(BF).astype(F32)
    second = (stats - first).astype(BF).astype(F32)
    third = stats - first - second
    pack_ref[:, E:] = (first + pltpu.roll(second, 2 * heads, 1) + pltpu.roll(third, 4 * heads, 1)).astype(BF)


def newton_body(land_ref, lmask_ref, kt_ref, mixer_ref, p_ref, w_ref, pi_ref):
    E = kt_ref.shape[1]
    eye = eye_row()
    allowed = jnp.concatenate([lmask_ref[...]] * PACK, 1) > 0.5
    for g in range(E // BLOCK):
        s = group(g)
        lq, lk = land_ref[:, s], land_ref[:, E + g * BLOCK : E + (g + 1) * BLOCK]
        z = nt(lk, expand(lq)) * SCALE
        z = jnp.where(allowed, z, -1e30)
        e = jnp.where(allowed, jnp.exp(z - jnp.max(z, axis=0, keepdims=True)), 0.0)
        kt = e / jnp.sum(e, axis=0, keepdims=True)
        inv = 1.0 / head_total(kt * kt)
        kt_ref[:, s] = kt
        p = tn3(kt, kt) * inv
        pi = None
        for step in range(NEWTON):
            p_ref[step, :, s] = p
            p2 = mm3(p, p)
            w = 0.25 * (13.0 * eye - 15.0 * p + mm3(p2, 7.0 * eye - p))
            w_ref[step, :, s] = w
            if step < NEWTON - 1:
                p = mm3(p, w)
            pi = w if pi is None else mm3(pi, w)
            pi_ref[step, :, s] = pi
        mixer_ref[:, s] = mm3(kt, pi) * inv


def newton_back_body(land_ref, kt_ref, p_ref, w_ref, pi_ref, mixer_ref, gmix_ref, lval_ref, lq_ref, lk_ref):
    E = kt_ref.shape[1]
    for g in range(E // BLOCK):
        s = group(g)
        lq, lk = land_ref[:, s], land_ref[:, E + g * BLOCK : E + (g + 1) * BLOCK]
        kt = kt_ref[:, s]
        inv = 1.0 / head_total(kt * kt)
        gh, gl = split(gmix_ref[:, s])
        vh, vl = split(lval_ref[:, s])
        wide = expand(vh)
        grad = nt(gh, wide) + nt(gl, wide) + nt(gh, expand(vl))
        d_pi = tn3(kt, grad) * inv
        d_kt = mm3(grad, pi_ref[NEWTON - 1, :, s]) * inv
        d_c = -head_total(grad * mixer_ref[:, s]) * inv
        d_p = None
        for step in reversed(range(NEWTON)):
            p, w = p_ref[step, :, s], w_ref[step, :, s]
            d_w = d_pi if step == 0 else mm3(pi_ref[step - 1, :, s], d_pi)
            if d_p is not None:
                d_w = d_w + mm3(p, d_p)
                d_p = mm3(d_p, w)
            if step > 0:
                d_pi = mm3(d_pi, w)
            a = mm3(p, d_w)
            ab = a + mm3(d_w, p)
            more = 0.25 * (7.0 * ab - 15.0 * d_w - mm3(p, a) - mm3(ab, p))
            d_p = more if d_p is None else d_p + more
        d_c = d_c - head_total(d_p * p_ref[0, :, s]) * inv
        d_s = d_p * inv
        kh, kl = split(kt)
        sh, sl = split(d_s)
        wide = expand(sh)
        thin = expand(sl)
        d_kt = d_kt + nn(kh, wide) + nn(kl, wide) + nn(kh, thin) + nt(kh, wide) + nt(kl, wide) + nt(kh, thin)
        d_kt = d_kt + 2.0 * d_c * kt
        dz = kt * (d_kt - jnp.sum(kt * d_kt, axis=0, keepdims=True)) * SCALE
        zh, zl = split(dz)
        wide = expand(lq)
        lk_ref[:, s] = nn(zh, wide) + nn(zl, wide)
        lq_ref[:, s] = compress(tn(zh, lk) + tn(zl, lk))


def mix_body(*refs):
    n = len(refs) - 7
    packs = refs[:n]
    mixer_ref, ktok_ref, conv_ref, mixing_ref, lval_ref, scale_ref, mixed_ref = refs[n:]
    E = mixer_ref.shape[1]
    heads = E // HEAD_DIM
    stats = []
    for p in packs:
        tile = p[:, E:].astype(F32)
        stats.append(tile + pltpu.roll(tile, 128 - 2 * heads, 1) + pltpu.roll(tile, 128 - 4 * heads, 1))
    top = stats[0]
    for t in stats[1:]:
        top = jnp.maximum(top, t)
    lane = lax.broadcasted_iota(jnp.int32, (HEAD_DIM, 128), 1)
    weights = [jnp.where(lane < heads, jnp.exp(jnp.minimum(t - top, 0.0)), 0.0) for t in stats]
    total = sum(w * pltpu.roll(t, 128 - heads, 1) for w, t in zip(weights, stats))
    total = jnp.where(lane < heads, total, 1.0)
    weights = [w / total for w in weights]
    scale_ref[...] = weights[0]
    head = lane_head(HEAD_DIM)
    for g in range(E // BLOCK):
        s = group(g)
        lval = jnp.zeros((HEAD_DIM, BLOCK), F32)
        for w, p in zip(weights, packs):
            spread = jnp.zeros((HEAD_DIM, BLOCK), F32)
            for i in range(PACK):
                h = g * PACK + i
                spread = jnp.where(head == i, w[:, h : h + 1], spread)
            lval = lval + spread * p[:, s].astype(F32)
        lval_ref[:, s] = lval
        mixing = mm3(mixer_ref[:, s], lval)
        mixing_ref[:, s] = mixing
        mh, ml = split(mixing)
        tok = ktok_ref[s, :]
        mixed_ref[:, s] = (tn(tok, expand(mh)) + tn(tok, expand(ml)) + conv_ref[:, s]).astype(BF)


def pair_pick(first, second):
    lane = lax.broadcasted_iota(jnp.int32, first.shape, 1)
    return jnp.where(lane < HEAD_DIM, first, second)


def band_apply(row, band, edge, a_ref, rim_ref, cols):
    T = a_ref.shape[0]
    wide = pltpu.roll(jnp.broadcast_to(row, (T, T)), 0, 1, stride=1, stride_axis=0)
    wide = jnp.where(band, wide, 0.0).astype(BF)
    short = jnp.broadcast_to(row, (REACH, T))
    rims = jnp.concatenate(
        [
            pltpu.roll(short, REACH, 1, stride=1, stride_axis=0),
            pltpu.roll(short, 0, 1, stride=1, stride_axis=0),
        ],
        0,
    )[:, :128]
    rims = jnp.where(edge, rims, 0.0).astype(BF)
    return nn(wide, a_ref[:, cols]), nn(rims, rim_ref[:, cols])


def conv_pair(rows_ref, band, edge, a_ref, rim_ref, out_ref, j):
    T = a_ref.shape[0]
    cols = slice(j * 128, (j + 1) * 128)
    one, one_rim = band_apply(rows_ref[2 * j : 2 * j + 1, :], band, edge, a_ref, rim_ref, cols)
    two, two_rim = band_apply(rows_ref[2 * j + 1 : 2 * j + 2, :], band, edge, a_ref, rim_ref, cols)
    both, rim = pair_pick(one, two), pair_pick(one_rim, two_rim)
    out_ref[:REACH, cols] = both[:REACH] + rim[:REACH]
    out_ref[REACH : T - REACH, cols] = both[REACH : T - REACH]
    out_ref[T - REACH :, cols] = both[T - REACH :] + rim[REACH:]


def conv_body(rows_ref, band_ref, edge_ref, v_ref, rim_ref, out_ref):
    band = band_ref[...] > 0.5
    edge = edge_ref[...] > 0.5
    for j in range(v_ref.shape[1] // 128):
        conv_pair(rows_ref, band, edge, v_ref, rim_ref, out_ref, j)


def conv_back_body(
    rows_ref, band_ref, edge_ref, band_rev_ref, edge_rev_ref, g_ref, g_rim_ref, v_ref, v_rim_ref, out_ref, tap_ref, tap_before_ref, tap_after_ref
):
    T = g_ref.shape[0]
    band = band_ref[...] > 0.5
    edge = edge_ref[...] > 0.5
    band_rev = band_rev_ref[...] > 0.5
    edge_rev = edge_rev_ref[...] > 0.5
    a = lax.broadcasted_iota(jnp.int32, (T, T), 0)
    b = lax.broadcasted_iota(jnp.int32, (T, T), 1)
    flip = jnp.where(a + b == T - 1, 1.0, 0.0).astype(BF)
    a = lax.broadcasted_iota(jnp.int32, (128, 128), 0)
    b = lax.broadcasted_iota(jnp.int32, (128, 128), 1)
    flip_before = jnp.where(a + b == REACH - 1, 1.0, 0.0).astype(BF)
    flip_after = jnp.where((a + b == 2 * REACH - 1) & (a < REACH), 1.0, 0.0).astype(BF)
    for j in range(g_ref.shape[1] // 128):
        cols = slice(j * 128, (j + 1) * 128)
        conv_pair(rows_ref, band, edge, g_ref, g_rim_ref, out_ref, j)
        v_rev = nn(flip, v_ref[:, cols]).astype(BF)
        before = nn(flip_before, v_rim_ref[:, cols]).astype(BF)
        after = nn(flip_after, v_rim_ref[:, cols]).astype(BF)
        g = g_ref[:, cols].astype(F32)
        lane = lax.broadcasted_iota(jnp.int32, g.shape, 1)
        for i in range(2):
            mine = jnp.where((lane < HEAD_DIM) == (i == 0), g, 0.0).astype(BF)
            h = 2 * j + i
            cross = jnp.where(band_rev, nt(mine, v_rev), 0.0)
            cross = pltpu.roll(cross, 0, 1, stride=1, stride_axis=0)
            tap_ref[h : h + 1, :] = jnp.sum(cross, axis=0, keepdims=True)
            low = jnp.where(edge_rev[:REACH], nt(mine[:REACH], before), 0.0)
            low = pltpu.roll(low, 0, 1, stride=1, stride_axis=0)
            tap_before_ref[h : h + 1, :] = jnp.sum(low, axis=0, keepdims=True)
            high = jnp.where(edge_rev[REACH:], nt(mine[T - REACH :], after), 0.0)
            high = pltpu.roll(high, 0, 1, stride=1, stride_axis=0)
            tap_after_ref[h : h + 1, :] = jnp.sum(high, axis=0, keepdims=True)


def gmix_body(ktok_ref, gm_ref, out_ref):
    for g in range(gm_ref.shape[1] // BLOCK):
        s = group(g)
        out_ref[:, s] = compress(nn(ktok_ref[s, :], gm_ref[:, s])).astype(BF)


def tok_back_body(ktok_ref, mixing_ref, gm_ref, q_ref, land_ref, gq_ref, lk_ref):
    E = gm_ref.shape[1]
    for g in range(E // BLOCK):
        s = group(g)
        lk = land_ref[:, E + g * BLOCK : E + (g + 1) * BLOCK]
        mh, ml = split(mixing_ref[:, s])
        gm = gm_ref[:, s]
        gk = nt(expand(mh), gm) + nt(expand(ml), gm)
        tok = ktok_ref[s, :].astype(F32)
        gz = (tok * (gk - heads_sum(tok * gk)) * SCALE).astype(BF)
        gq_ref[:, s] = tn(gz, expand(lk))
        lk_ref[:, s] = compress(nn(gz, q_ref[:, s]))


def key_back_body(*refs):
    n = len(refs) - 12
    gmixes = refs[:n]
    mixer_ref, lval_ref, ekey_ref, scale_ref, v_ref, k_ref, land_ref, gvc_ref, gmix_ref, gv_ref, gk_ref, lq_ref = refs[n:]
    E = v_ref.shape[1]
    for g in range(E // BLOCK):
        s = group(g)
        gmix = gmixes[0][:, s].astype(F32)
        for other in gmixes[1:]:
            gmix = gmix + other[:, s].astype(F32)
        gmix_ref[:, s] = gmix
        lval = lval_ref[:, s]
        glval = tn3(mixer_ref[:, s], gmix)
        gh, gl = split(glval)
        wide = expand(gh)
        v = v_ref[:, s]
        gkk = nt(wide, v) + nt(expand(gl), v)
        center = jnp.sum(expand(glval * lval), axis=1, keepdims=True)
        scale = jnp.concatenate([scale_ref[:, g * PACK + i : g * PACK + i + 1] for i in range(PACK)], 0)
        kk = ekey_ref[s, :].astype(F32) * scale
        gz = (kk * (gkk - center) * SCALE).astype(BF)
        gv_ref[:, s] = (tn(kk.astype(BF), wide) + gvc_ref[:, s]).astype(BF)
        gk_ref[:, s] = tn(gz, expand(land_ref[:, s]))
        lq_ref[:, s] = compress(nn(gz, k_ref[:, s]))


def call(body, outs, *args, flops=2e9):
    shapes = [jax.ShapeDtypeStruct(*o) for o in outs]
    size = sum(a.size * a.dtype.itemsize for a in args) + sum(a.size * a.dtype.itemsize for a in shapes)
    return pl.pallas_call(
        body,
        out_shape=shapes,
        compiler_params=pltpu.CompilerParams(vmem_limit_bytes=40 << 20),
        cost_estimate=pl.CostEstimate(flops=int(flops), bytes_accessed=size, transcendentals=0),
        name=body.__name__,
    )(*args)


def norm_rows(rows, gain, shift):
    center = rows - jnp.mean(rows, axis=-1, keepdims=True)
    spread = jnp.mean(center * center, axis=-1, keepdims=True)
    return center * lax.rsqrt(spread + EPS) * gain + shift


def local(x_in, out_cot, seg_ids, land_doc, w_qkv, w_out, w_up, w_down, conv_taps, head_bias, ffn_bias, gains, offsets):
    nf, nc, nt = lax.axis_size("fsdp"), lax.axis_size("ctx"), lax.axis_size("tp")
    f_i, c_i, t_i = lax.axis_index("fsdp"), lax.axis_index("ctx"), lax.axis_index("tp")
    assert nt == 2 and x_in.shape[0] == 2
    ctx_bits = [("ctx", 1 << b) for b in range(nc.bit_length() - 1)]
    chip_bits = [("fsdp", 1 << b) for b in range(1, nf.bit_length() - 1)]
    core_bits = [("fsdp", 1)]
    row_bits = ctx_bits + chip_bits + core_bits
    T, D = x_in.shape[1:]
    R = w_qkv.shape[0]
    C = w_qkv.shape[2]
    FL = w_up.shape[1]
    HL = C // HEAD_DIM
    H = 2 * HL
    LL = land_doc.shape[1]
    L = LL * nc
    seg_len = T // LL

    q_pos = jnp.arange(D, dtype=jnp.int32)
    piece, inner = q_pos // R, q_pos % R
    mf = jnp.zeros_like(piece)
    mc = jnp.zeros_like(piece)
    for i, (axis, mask) in enumerate(row_bits):
        bit = ((piece >> i) & 1) * mask
        if axis == "fsdp":
            mf = mf ^ bit
        else:
            mc = mc ^ bit
    true_pos = ((f_i ^ mf) * nc + (c_i ^ mc)) * R + inner
    perm = (jnp.arange(D, dtype=jnp.int32)[:, None] == true_pos[None, :]).astype(BF)

    def pick(a):
        return lax.dynamic_index_in_dim(a, t_i, 0, False)

    seg = pick(seg_ids)
    doc = pick(land_doc)
    x = dot("td,dq->tq", pick(x_in), perm).astype(BF)
    cot = dot("td,dq->tq", pick(out_cot), perm).astype(BF)
    vec = hdot("vd,dq->vq", jnp.concatenate([gains, offsets], 0), perm.astype(F32))
    gain = vec[:2]
    shift = vec[2:]

    up = [(i, i + 1) for i in range(nc - 1)]
    down = [(i + 1, i) for i in range(nc - 1)]
    seg_before = jnp.where(c_i == 0, -1, lax.ppermute(seg[T - REACH :], "ctx", up))
    seg_after = jnp.where(c_i == nc - 1, -1, lax.ppermute(seg[:REACH], "ctx", down))
    docs = doc[None]
    for bit in ctx_bits:
        docs = grow(docs, bit)
    l_pos = jnp.arange(L, dtype=jnp.int32)
    l_true = (c_i ^ (l_pos // LL)) * LL + l_pos % LL
    l_perm = l_pos[:, None] == l_true[None, :]
    docs = jnp.sum(jnp.where(l_perm, docs.reshape(1, L), 0), axis=1)
    par = jnp.concatenate([conv_taps.reshape(-1), head_bias.reshape(-1), ffn_bias.reshape(-1)])
    par2 = jnp.stack([par, swap(par, "tp", 1)])
    taps = par2[:, : KW * HL].reshape(2, KW, HL).transpose(1, 0, 2).reshape(KW, H)
    hb = par2[:, KW * HL : KW * HL + 2 * C].reshape(2, 2, C).transpose(1, 0, 2).reshape(2, 2 * C)
    fb = par2[:, KW * HL + 2 * C :].reshape(2 * FL)

    def gather(pack):
        for bit in ctx_bits:
            pack = grow(pack, bit)
        half = pack.shape[1] // 2
        one, two = pack[:, :half], pack[:, half:]
        for bit in chip_bits:
            one = grow(one, bit)
        one = jnp.concatenate([one, swap(one, "tp", 1)], axis=1)
        two = jnp.concatenate([two, swap(two, "tp", 1)], axis=1)
        for bit in chip_bits:
            two = grow(two, bit)
        return grow(one, core_bits[0]), grow(two, core_bits[0])

    w1, w2 = gather(jnp.concatenate([w_qkv.reshape(R, 3 * C), w_out], axis=1))
    wu, wd = gather(jnp.concatenate([w_up, w_down], axis=1))
    wq = jnp.concatenate([w1[:, :C], w1[:, 2 * C : 3 * C]], 1)
    wk = jnp.concatenate([w1[:, C : 2 * C], w1[:, 3 * C :]], 1)
    wv = jnp.concatenate([w2[:, :C], w2[:, 2 * C : 3 * C]], 1)
    wo = jnp.concatenate([w2[:, C : 2 * C], w2[:, 3 * C :]], 1)

    q = (dot("td,de->te", x, wq) + hb[0]).astype(BF)
    k = dot("td,de->te", x, wk).astype(BF)
    v = (dot("td,de->te", x, wv) + hb[1]).astype(BF)
    E = q.shape[1]
    mean_mat = (jnp.arange(T)[:, None] // seg_len == jnp.arange(LL)[None, :]).astype(BF) / seg_len
    piece0 = jnp.concatenate([dot("ta,te->ae", mean_mat, q), dot("ta,te->ae", mean_mat, k)], 1).astype(BF)

    def rims(a):
        before = lax.ppermute(a[T - REACH :], "ctx", up)
        after = lax.ppermute(a[:REACH], "ctx", down)
        return jnp.concatenate([before, after, jnp.zeros((128 - 2 * REACH, a.shape[1]), a.dtype)], 0)

    pieces = [piece0] + [swap(piece0, "ctx", p) for p in range(1, nc)]
    land = jnp.concatenate(
        [sum(jnp.where((c_i ^ p) == a, pieces[p], 0) for p in range(nc)) for a in range(nc)], 0
    ).astype(BF)
    mask = (docs[:, None] == seg[None, :]).astype(F32)
    lmask = (docs[:, None] == docs[None, :]).astype(F32)
    ktok, ekey, pack = call(scores_body, [((E, T), BF), ((E, T), BF), ((L, E + 128), BF)], q, k, v, land, mask)
    packs = [pack] + [swap(pack, "ctx", p) for p in range(1, nc)]
    v_rim = rims(v)
    kt, mixer, p_all, w_all, pi_all = call(
        newton_body,
        [((L, E), F32), ((L, E), F32)] + [((NEWTON, L, E), F32)] * 3,
        land,
        lmask,
    )

    t_pos = jnp.arange(T)
    diff = t_pos[None, :] - t_pos[:, None]
    band = ((jnp.abs(diff) <= REACH) & (seg[None, :] == seg[:, None])).astype(F32)
    r_pos = jnp.arange(REACH)
    edge_before = (r_pos[None, :] >= r_pos[:, None]) & (seg_before[None, :] == seg[:REACH, None])
    edge_after = (r_pos[None, :] <= r_pos[:, None]) & (seg_after[None, :] == seg[T - REACH :, None])
    none = jnp.zeros((REACH, REACH), bool)
    zero = jnp.zeros((2 * REACH, 128 - 2 * REACH), F32)
    edge = jnp.concatenate(
        [jnp.concatenate([jnp.concatenate([edge_before, none], 1), jnp.concatenate([none, edge_after], 1)], 0).astype(F32), zero], 1
    )
    gap = jnp.zeros((H, T - KW), F32)
    tap_t = taps.T
    row_fwd = jnp.concatenate([tap_t[:, REACH:], gap, tap_t[:, :REACH]], 1)
    tap_r = tap_t[:, ::-1]
    row_back = jnp.concatenate([tap_r[:, REACH:], gap, tap_r[:, :REACH]], 1)
    (conv,) = call(conv_body, [((T, E), F32)], row_fwd, band, edge, v, v_rim)
    mixing, lval, land_scale, mixed = call(
        mix_body, [((L, E), F32), ((L, E), F32), ((L, 128), F32), ((T, E), BF)], *packs, mixer, ktok, conv
    )

    branch = dot("te,de->td", mixed, wo) + shift[2]
    hidden, pull_first = jax.vjp(norm_rows, x.astype(F32) + branch, gain[0], shift[0])
    hidden_low = hidden.astype(BF)
    upward = dot("td,df->tf", hidden_low, wu) + fb
    active, gelu_pull = jax.vjp(lambda u: jax.nn.gelu(u, approximate=True), upward)
    active_low = active.astype(BF)
    ffn = dot("tf,df->td", active_low, wd) + shift[3]
    output, pull_second = jax.vjp(norm_rows, hidden + ffn, gain[1], shift[1])
    grad_second, gain_second, shift_second = pull_second(cot.astype(F32))
    grad_ffn = grad_second.astype(BF)
    d_down = dot("td,tf->df", grad_ffn, active_low).astype(BF)
    grad_up = gelu_pull(dot("td,df->tf", grad_ffn, wd))[0].astype(BF)
    d_up = dot("td,tf->df", hidden_low, grad_up).astype(BF)
    grad_hidden = dot("tf,df->td", grad_up, wu) + grad_second
    grad_first, gain_first, shift_first = pull_first(grad_hidden)
    grad_branch = grad_first.astype(BF)
    d_out = dot("td,te->de", grad_branch, mixed).astype(BF)
    gm = dot("td,de->te", grad_branch, wo).astype(BF)

    def scatter(one, two):
        one = shrink(one, core_bits[0])
        two = shrink(two, core_bits[0])

        def fold(a):
            half = a.shape[1] // 2
            return (a[:, :half].astype(F32) + swap(a[:, half:], "tp", 1).astype(F32)).astype(BF)

        one = fold(one)
        for bit in reversed(chip_bits):
            one = shrink(one, bit)
        for bit in reversed(chip_bits):
            two = shrink(two, bit)
        two = fold(two)
        both = jnp.concatenate([one, two], 1)
        for bit in reversed(ctx_bits):
            both = shrink(both, bit)
        return both.astype(F32)

    ud = scatter(d_up, d_down)

    (gmix0,) = call(gmix_body, [((L, E), BF)], ktok, gm)
    gmixes = [gmix0] + [swap(gmix0, "ctx", p) for p in range(1, nc)]
    gm_rim = rims(gm)
    gq, lk_part = call(tok_back_body, [((T, E), F32), ((L, E), F32)], ktok, mixing, gm, q, land)
    band_rev = band[:, ::-1]
    zero = jnp.zeros((REACH, 128 - REACH), F32)
    edge_rev = jnp.concatenate(
        [jnp.concatenate([edge_before[:, ::-1].astype(F32), zero], 1), jnp.concatenate([edge_after[:, ::-1].astype(F32), zero], 1)], 0
    )
    gvc, tap_main, tap_before, tap_after = call(
        conv_back_body,
        [((T, E), F32), ((H, T), F32), ((H, 128), F32), ((H, 128), F32)],
        row_back, band, edge, band_rev, edge_rev, gm, gm_rim, v, v_rim,
    )
    tap_grad = jnp.concatenate([tap_main[:, REACH - 1 :: -1], tap_main[:, : T - REACH - 2 : -1]], 1)
    tap_grad = tap_grad + jnp.concatenate([tap_before[:, REACH - 1 :: -1], tap_after[:, 2 * REACH - 1 : REACH - 2 : -1]], 1)
    tap_grad = tap_grad.T
    gmix, gv, gk, lq_part = call(
        key_back_body, [((L, E), F32), ((T, E), BF), ((T, E), F32), ((L, E), F32)],
        *gmixes, mixer, lval, ekey, land_scale, v, k, land, gvc,
    )
    lq_mix, lk_mix = call(
        newton_back_body, [((L, E), F32), ((L, E), F32)], land, kt, p_all, w_all, pi_all, mixer, gmix, lval
    )
    part = jnp.concatenate([lq_part, lk_part], 1).reshape(nc, LL, 2 * E)
    lmix = jnp.concatenate([lq_mix, lk_mix], 1).reshape(nc, LL, 2 * E)

    def piece_of(a, p):
        return lax.dynamic_index_in_dim(a, c_i ^ p, 0, False)

    own = piece_of(part, 0) + piece_of(lmix, 0)
    for p in range(1, nc):
        own = own + swap(piece_of(part, p).astype(BF), "ctx", p).astype(F32)
    spread = jnp.repeat(own / seg_len, seg_len, axis=0)
    gq = (gq + spread[:, :E]).astype(BF)
    gk = (gk + spread[:, E:]).astype(BF)
    d_q = dot("td,te->de", x, gq).astype(BF)
    d_k = dot("td,te->de", x, gk).astype(BF)
    d_v = dot("td,te->de", x, gv).astype(BF)
    d1 = jnp.concatenate([d_q[:, :C], d_k[:, :C], d_q[:, C:], d_k[:, C:]], 1)
    d2 = jnp.concatenate([d_v[:, :C], d_out[:, :C], d_v[:, C:], d_out[:, C:]], 1)
    qo = scatter(d1, d2)
    gx = dot("te,de->td", gq, wq) + dot("te,de->td", gk, wk) + dot("te,de->td", gv, wv) + grad_first

    hb_grad = jnp.stack([jnp.sum(gq.astype(F32), 0), jnp.sum(gv.astype(F32), 0)])
    fb_grad = jnp.sum(grad_up.astype(F32), 0)
    vec_grad = jnp.stack(
        [gain_first, gain_second, shift_first, shift_second, jnp.sum(grad_branch.astype(F32), 0), jnp.sum(grad_ffn.astype(F32), 0)]
    )
    vec_grad = hdot("vq,dq->vd", vec_grad, perm.astype(F32)).reshape(-1)

    def side(s):
        return jnp.concatenate(
            [tap_grad[:, s * HL : (s + 1) * HL].reshape(-1), hb_grad[:, s * C : (s + 1) * C].reshape(-1), fb_grad[s * FL : (s + 1) * FL]]
        )

    small = jnp.concatenate([side(0), vec_grad])
    small = small + swap(jnp.concatenate([side(1), vec_grad]), "tp", 1)
    for bit in row_bits:
        small = small + swap(small, *bit)
    n0, n1, n2 = KW * HL, KW * HL + 2 * C, KW * HL + 2 * C + FL
    vec_sum = small[n2:].reshape(6, D)

    def place(rows):
        mine = dot("tq,dq->td", rows.astype(BF), perm).astype(BF)
        other = swap(mine, "tp", 1)
        first = t_i == 0
        return jnp.stack([jnp.where(first, mine, other), jnp.where(first, other, mine)])

    return (
        place(output),
        place(gx),
        qo[:, : 3 * C].reshape(R, 3, C),
        qo[:, 3 * C :],
        ud[:, :FL],
        ud[:, FL:],
        small[:n0].reshape(KW, HL),
        small[n0:n1].reshape(2, C),
        small[n1:n2],
        vec_sum[:2],
        vec_sum[2:],
    )


def solution(mesh):
    placed = (
        P("fsdp", "ctx", None),
        P("fsdp", "ctx", None),
        P("fsdp", "ctx"),
        P("fsdp", "ctx"),
        P(("fsdp", "ctx"), None, "tp"),
        P(("fsdp", "ctx"), "tp"),
        P(("fsdp", "ctx"), "tp"),
        P(("fsdp", "ctx"), "tp"),
        P(None, "tp"),
        P(None, "tp"),
        P("tp"),
        P(),
        P(),
    )
    return jax.shard_map(
        local,
        mesh=mesh,
        in_specs=placed,
        out_specs=placed[:2] + placed[4:],
        check_vma=False,
    )
```

time: 1290 us -> 400 us (0.31)
  waiting for transfers between devices: 584 us -> 155 us
  blocking collectives: 338 us -> 0 us
  matrix products: 168 us -> 40.1 us
  other arithmetic: 84.8 us -> 32.2 us
  starting transfers between devices: 15.5 us -> 67.1 us
  Pallas kernels: 0 us -> 42.3 us
  local copies, waits for them, and re-layouts: 66.6 us -> 52.7 us
  between operations: 16.1 us -> 2.91 us
    reduce_scatter x8 -> x0, waiting for transfers between devices: 257 us -> none  [the longest x1 79.5 us: local(): lax.psum_scatter(big_total[3], ('fsdp', 'ctx'), scatter_dimension=0, tile...]
    all_gather x14 -> x0, blocking collectives: 233 us -> none  [the longest x2 78.2 us: local(): lax.all_gather(w_out, ('fsdp', 'ctx'), axis=0, tiled=True)]
    all_gather x6 -> x0, waiting for transfers between devices: 165 us -> none  [the longest x2 84.4 us: local(): lax.all_gather(w_up, ('fsdp', 'ctx'), axis=0, tiled=True)]
    psum x8 -> x0, waiting for transfers between devices: 156 us -> none  [head_sum(): lax.psum(partial_value.astype(jnp.bfloat16), 'tp').astype(jnp.float32)]
    ppermute x8 -> x60, waiting for transfers between devices: 0.02 us -> 155 us  [the longest x54 154 us: swap(): lax.ppermute(a, axis, [(i, i ^ mask) for i in range(lax.axis_size(axis))])]
    dot_general x204 -> x25, matrix products: 168 us -> 40.1 us  [the longest x23 37.4 us: dot(): return jnp.einsum(spec, a, b, preferred_element_type=F32)]
    psum x3 -> x0, blocking collectives: 105 us -> none  [the longest x1 62.4 us: local(): lax.psum((small_total[0], small_total[1], small_total[2], small_total[3],...]
    ppermute x8 -> x60, starting transfers between devices: 14.6 us -> 67.1 us  [the longest x54 48.7 us: swap(): lax.ppermute(a, axis, [(i, i ^ mask) for i in range(lax.axis_size(axis))])]
  transfers between devices with their start and end apart: 30 -> 60, of which waited for: 20 -> 24; matrix products, arithmetic and copies ran while one was open for 11% -> 23% of each run, Pallas kernels for 0% -> 11%
where the time goes in v1:
time: 400 us; the launch traced here: 393 us
  waiting for transfers between devices  155 us (39%)
  starting transfers between devices  67.1 us (17%)
  local copies, waits for them, and re-layouts  52.7 us (13%)
  Pallas kernels  42.3 us (11%)
  matrix products  40.1 us (10%)
  other arithmetic  32.2 us (8%)
    ppermute x54, waiting for transfers between devices, swap(): lax.ppermute(a, axis, [(i, i ^ mask) for i in range(lax.axis_size(axis))])  154 us
    ppermute x54, starting transfers between devices, swap(): lax.ppermute(a, axis, [(i, i ^ mask) for i in range(lax.axis_size(axis))])  48.7 us
    pallas_call x9, Pallas kernels, call(): pl.pallas_call(body, out_shape=shapes, compiler_params=pltpu.CompilerPara...  42.3 us
    dot_general x23, matrix products, dot(): return jnp.einsum(spec, a, b, preferred_element_type=F32)  37.4 us
    unnamed x170, local copies, waits for them, and re-layouts  21.1 us
    convert_element_type x10, other arithmetic, shrink(): return (a[:half].astype(F32) + got.astype(F32)).astype(a.dtype)  10.3 us
    ppermute x2, starting transfers between devices, rims(): before = lax.ppermute(a[T - REACH:], 'ctx', up)  10.1 us
    slice x11, local copies, waits for them, and re-layouts, shrink(): got = swap(a[half:], *bit)  9.12 us
  transfers between devices with their start and end apart: 60, of which 24 were waited for; matrix products, arithmetic and copies ran while one was open for 23% of the time, Pallas kernels for 11%

profile of v1, /device:TPU:0, one launch (start us, length us, event | category | flops | bytes accessed | tf_op | source)
XLA Modules:
  0.0 392.8 jit_solution(12544137586598010581)
XLA Ops:
  23.3 4.5 %collective-permute-start.17 = (s32[16]{0:T(128)S(1)}, s32[16]{0:T(128)S(1)}, u32[]{:S(2)}, u32[]{:S(2)}) collective-permute-start(s32[16]{0:T(128)S(1)} %get-tuple-element.177), channel_id=1, source_target_pairs={{0,2},{2,4},{4,6},{1,3},{3,5},{5,7},{8,10},{10,12},{12,14},{9,11},... | collective-permute-start | bytes 200 | tf_op jit(solution)/shard_map/ppermute | solution.py:447
  38.4 9.6 %collective-permute-done.1 = bf16[96,1536]{1,0:T(8,128)(2,1)S(1)} collective-permute-done((bf16[96,1536]{1,0:T(8,128)(2,1)S(1)}, bf16[96,1536]{1,0:T(8,128)(2,1)S(1)}, u32[]{:S(2)}, u32[]{:S(2)}) %collective-permute-start.1) | collective-permute-done | bytes 294944 | tf_op jit(solution)/shard_map/ppermute | solution.py:30
  50.4 5.4 %collective-permute-done.2 = bf16[192,768]{1,0:T(8,128)(2,1)S(1)} collective-permute-done((bf16[192,768]{1,0:T(8,128)(2,1)S(1)}, bf16[192,768]{1,0:T(8,128)(2,1)S(1)}, u32[]{:S(2)}, u32[]{:S(2)}) %collective-permute-start.2) | collective-permute-done | bytes 294944 | tf_op jit(solution)/shard_map/ppermute | solution.py:30
  59.0 18.0 %collective-permute-done.22 = bf16[96,3072]{1,0:T(8,128)(2,1)S(1)} collective-permute-done((bf16[96,3072]{1,0:T(8,128)(2,1)S(1)}, bf16[96,3072]{1,0:T(8,128)(2,1)S(1)}, u32[]{:S(2)}, u32[]{:S(2)}) %collective-permute-start.22) | collective-permute-done | bytes 589856 | tf_op jit(solution)/shard_map/ppermute | solution.py:30
  81.4 10.5 %collective-permute-done.26 = bf16[192,1536]{1,0:T(8,128)(2,1)} collective-permute-done((bf16[192,1536]{1,0:T(8,128)(2,1)S(1)}, bf16[192,1536]{1,0:T(8,128)(2,1)}, u32[]{:S(2)}, u32[]{:S(2)}) %collective-permute-start.26) | collective-permute-done | bytes 589856 | tf_op jit(solution)/shard_map/ppermute | solution.py:30
  105.2 4.8 %collective-permute-start.19 = (bf16[16,768]{1,0:T(8,128)(2,1)S(1)}, bf16[16,768]{1,0:T(8,128)(2,1)S(1)}, u32[]{:S(2)}, u32[]{:S(2)}) collective-permute-start(bf16[16,768]{1,0:T(8,128)(2,1)S(1)} %get-tuple-element.159), channel_id=1, source_target_pairs={{0,2},{2,4},{4,6},{1,3},{3,5},{5,7},{8,10},{10,12},{12,14},{9,11},... | collective-permute-start | bytes 73736 | tf_op jit(solution)/shard_map/ppermute | solution.py:490
  116.6 6.2 %collective-permute-done.24 = bf16[384,1536]{1,0:T(8,128)(2,1)S(1)} collective-permute-done((bf16[384,1536]{1,0:T(8,128)(2,1)S(1)}, bf16[384,1536]{1,0:T(8,128)(2,1)S(1)}, u32[]{:S(2)}, u32[]{:S(2)}) %collective-permute-start.24) | collective-permute-done | bytes 1179680 | tf_op jit(solution)/shard_map/ppermute | solution.py:30
  130.7 13.9 %newton_body.1 = (f32[64,768]{1,0:T(8,128)S(1)}, f32[64,768]{1,0:T(8,128)S(1)}, f32[6,64,768]{2,1,0:T(8,128)S(1)}, f32[6,64,768]{2,1,0:T(8,128)S(1)}, f32[6,64,768]{2,1,0:T(8,128)S(1)}) custom-call(bf16[64,1536]{1,0:T(8,128)(2,1)S(1)} %pad_maximum_fusion.43.land_ref.refs_10_, f32[64,64]{1,0:T(8,128)S(1)} %compare_convert_fusion.1.lmask_ref), custom_call_target="tpu_custom_call" | custom-call | flops 2000000000 | bytes 4145152 | tf_op jit(solution)/shard_map/newton_body/pallas_call | solution.py:388
  151.4 4.1 %fusion.132 = (f32[256]{0:T(256)S(1)}, f32[256,768]{1,0:T(8,128)S(1)}) fusion(f32[768]{0:T(1024)S(1)} %copy-done.72, bf16[384,3072]{1,0:T(8,128)(2,1)S(1)} %collective-permute-done.28, bf16[192,3072]{1,0:T(8,128)(2,1)S(1)} %collective-permute-done.27, bf16[192,1536]{1,0:T(8,128)(2,1)} %collective-permute-done.26, bf16[192,1536]{1,0:T(8,128)(2,1)S(1)} %copy-done.31, ...), kind=kOutput, calls=%fused_computation.291 | convolution fusion | flops 1235287808 | bytes 9449472 | tf_op jit(solution)/shard_map/tf,df->td/dot_general | solution.py:22
  157.1 5.2 %convert_reduce_fusion = (f32[3072]{0:T(1024)S(1)}, bf16[256,3072]{1,0:T(8,128)(2,1)S(1)}) fusion(f32[256,3072]{1,0:T(8,128)S(1)} %convolution_add_fusion, bf16[256,768]{1,0:T(8,128)(2,1)S(1)} %get-tuple-element.118, bf16[384,3072]{1,0:T(8,128)(2,1)S(1)} %collective-permute-done.28, bf16[192,3072]{1,0:T(8,128)(2,1)S(1)} %collective-permute-done.27, ...), kind=kOutput, calls=%fused_computation.16 | convolution fusion | flops 1244132352 | bytes 9842688 | tf_op jit(solution)/shard_map/td,df->tf/dot_general | solution.py:22
  170.3 3.8 convolution_convert_fusion
  174.1 3.7 convolution_convert_fusion.1
  180.7 5.3 %collective-permute-start.33 = (bf16[16,768]{1,0:T(8,128)(2,1)S(1)}, bf16[16,768]{1,0:T(8,128)(2,1)}, u32[]{:S(2)}, u32[]{:S(2)}) collective-permute-start(bf16[16,768]{1,0:T(8,128)(2,1)S(1)} %get-tuple-element.157), channel_id=1, source_target_pairs={{0,2},{2,4},{4,6},{1,3},{3,5},{5,7},{8,10},{10,12},{12,14},{9,11},... | collective-permute-start | bytes 73736 | tf_op jit(solution)/shard_map/ppermute | solution.py:490
  214.4 3.5 collective-permute-start.35
  218.6 17.8 %newton_back_body.1 = (f32[64,768]{1,0:T(8,128)S(1)}, f32[64,768]{1,0:T(8,128)S(1)}) custom-call(bf16[64,1536]{1,0:T(8,128)(2,1)S(1)} %pad_maximum_fusion.43.land_ref.refs_10_, f32[64,768]{1,0:T(8,128)S(1)} %copy-done.13, f32[6,64,768]{2,1,0:T(8,128)S(1)} %copy-done.5, f32[6,64,768]{2,1,0:T(8,128)S(1)} %copy-done.7, f32[6,64,768]{2,1,0:T(8,128)S(1)} %copy-done.9, ...), custom_call_target="tpu_custom_call" | custom-call | flops 2000000000 | bytes 4915200 | tf_op jit(solution)/shard_map/newton_back_body/pallas_call | solution.py:388
  244.7 3.7 fusion.23
  254.5 4.2 %collective-permute-done.57 = f32[7110]{0:T(1024)S(1)} collective-permute-done((f32[7110]{0:T(1024)S(1)}, f32[7110]{0:T(1024)S(1)}, u32[]{:S(2)}, u32[]{:S(2)}) %collective-permute-start.57) | collective-permute-done | bytes 28472 | tf_op jit(solution)/shard_map/ppermute | solution.py:30
  283.3 8.8 %collective-permute-done.43 = bf16[192,1536]{1,0:T(8,128)(2,1)} collective-permute-done((bf16[192,1536]{1,0:T(8,128)(2,1)}, bf16[192,1536]{1,0:T(8,128)(2,1)}, u32[]{:S(2)}, u32[]{:S(2)}) %collective-permute-start.43) | collective-permute-done | bytes 589856 | tf_op jit(solution)/shard_map/ppermute | solution.py:30
  310.3 22.4 %collective-permute-done.51 = bf16[192,3072]{1,0:T(8,128)(2,1)S(1)} collective-permute-done((bf16[192,3072]{1,0:T(8,128)(2,1)S(1)}, bf16[192,3072]{1,0:T(8,128)(2,1)S(1)}, u32[]{:S(2)}, u32[]{:S(2)}) %collective-permute-start.51) | collective-permute-done | bytes 1179680 | tf_op jit(solution)/shard_map/ppermute | solution.py:30
  335.6 10.3 %collective-permute-done.52 = bf16[192,1536]{1,0:T(8,128)(2,1)S(1)} collective-permute-done((bf16[192,1536]{1,0:T(8,128)(2,1)S(1)}, bf16[192,1536]{1,0:T(8,128)(2,1)S(1)}, u32[]{:S(2)}, u32[]{:S(2)}) %collective-permute-start.52) | collective-permute-done | bytes 589856 | tf_op jit(solution)/shard_map/ppermute | solution.py:30
  347.8 17.1 %collective-permute-done.45 = bf16[96,1536]{0,1:T(8,128)(2,1)S(1)} collective-permute-done((bf16[96,1536]{0,1:T(8,128)(2,1)S(1)}, bf16[96,1536]{0,1:T(8,128)(2,1)S(1)}, u32[]{:S(2)}, u32[]{:S(2)}) %collective-permute-start.45) | collective-permute-done | bytes 294944 | tf_op jit(solution)/shard_map/ppermute | solution.py:30
  365.3 11.5 %collective-permute-done.53 = bf16[96,3072]{1,0:T(8,128)(2,1)S(1)} collective-permute-done((bf16[96,3072]{1,0:T(8,128)(2,1)S(1)}, bf16[96,3072]{1,0:T(8,128)(2,1)S(1)}, u32[]{:S(2)}, u32[]{:S(2)}) %collective-permute-start.53) | collective-permute-done | bytes 589856 | tf_op jit(solution)/shard_map/ppermute | solution.py:30
  377.1 8.2 %collective-permute-done.46 = bf16[48,1536]{0,1:T(8,128)(2,1)S(1)} collective-permute-done((bf16[48,1536]{0,1:T(8,128)(2,1)S(1)}, bf16[48,1536]{0,1:T(8,128)(2,1)S(1)}, u32[]{:S(2)}, u32[]{:S(2)}) %collective-permute-start.46) | collective-permute-done | bytes 147488 | tf_op jit(solution)/shard_map/ppermute | solution.py:30
  387.0 4.4 %collective-permute-done.54 = bf16[48,3072]{1,0:T(8,128)(2,1)S(1)} collective-permute-done((bf16[48,3072]{1,0:T(8,128)(2,1)S(1)}, bf16[48,3072]{1,0:T(8,128)(2,1)S(1)}, u32[]{:S(2)}, u32[]{:S(2)}) %collective-permute-start.54) | collective-permute-done | bytes 294944 | tf_op jit(solution)/shard_map/ppermute | solution.py:30
  (488 shorter events, 182.9 us)
Async XLA Ops:
  2.6 47.1 %collective-permute-start.21 = (bf16[48,3072]{1,0:T(8,128)(2,1)S(1)}, bf16[48,3072]{1,0:T(8,128)(2,1)S(1)}, u32[]{:S(2)}, u32[]{:S(2)}) collective-permute-start(bf16[48,3072]{1,0:T(8,128)(2,1)S(1)} %constant_dynamic-update-slice_fusion.2), channel_id=1, source_target_pairs={{0,2},{2,0},{4,6},{6,4},{1,3},{3,1},{5,7},{7,5},{8,10},{10,8},{12,... | collective-permute-start | bytes 884744 | tf_op jit(solution)/shard_map/ppermute | solution.py:30
  8.0 26.3 %collective-permute-start.5 = (f32[2502]{0:T(1024)S(1)}, f32[2502]{0:T(1024)S(1)}, u32[]{:S(2)}, u32[]{:S(2)}) collective-permute-start(f32[2502]{0:T(1024)S(1)} %concatenate.164), channel_id=1, source_target_pairs={{0,1},{1,0},{2,3},{3,2},{4,5},{5,4},{6,7},{7,6},{8,9},{9,8},{10,11... | collective-permute-start | bytes 30032 | tf_op jit(solution)/shard_map/ppermute | solution.py:30
  11.3 23.9 %collective-permute-start = (bf16[48,1536]{1,0:T(8,128)(2,1)S(1)}, bf16[48,1536]{1,0:T(8,128)(2,1)S(1)}, u32[]{:S(2)}, u32[]{:S(2)}) collective-permute-start(bf16[48,1536]{1,0:T(8,128)(2,1)S(1)} %constant_dynamic-update-slice_fusion), channel_id=1, source_target_pairs={{0,2},{2,0},{4,6},{6,4},{1,3},{3,1},{5,7},{7,5},{8,10},{10,8},{12,... | collective-permute-start | bytes 442376 | tf_op jit(solution)/shard_map/ppermute | solution.py:30
  49.7 27.3 %collective-permute-start.22 = (bf16[96,3072]{1,0:T(8,128)(2,1)S(1)}, bf16[96,3072]{1,0:T(8,128)(2,1)S(1)}, u32[]{:S(2)}, u32[]{:S(2)}) collective-permute-start(bf16[96,3072]{1,0:T(8,128)(2,1)S(1)} %pad_maximum_fusion.38), channel_id=1, source_target_pairs={{0,4},{2,6},{4,0},{6,2},{1,5},{3,7},{5,1},{7,3},{8,12},{10,14},{12... | collective-permute-start | bytes 1769480 | tf_op jit(solution)/shard_map/ppermute | solution.py:30
  55.9 21.9 %collective-permute-start.3 = (bf16[384,768]{1,0:T(8,128)(2,1)S(1)}, bf16[384,768]{1,0:T(8,128)(2,1)S(1)}, u32[]{:S(2)}, u32[]{:S(2)}) collective-permute-start(bf16[384,768]{1,0:T(8,128)(2,1)S(1)} %pad_maximum_fusion.36), channel_id=1, source_target_pairs={{0,1},{1,0},{2,3},{3,2},{4,5},{5,4},{6,7},{7,6},{8,9},{9,8},{10,11... | collective-permute-start | bytes 1769480 | tf_op jit(solution)/shard_map/ppermute | solution.py:30
  93.0 30.1 %collective-permute-start.27 = (bf16[192,3072]{1,0:T(8,128)(2,1)S(1)}, bf16[192,3072]{1,0:T(8,128)(2,1)S(1)}, u32[]{:S(2)}, u32[]{:S(2)}) collective-permute-start(bf16[192,3072]{1,0:T(8,128)(2,1)S(1)} %pad_maximum_fusion.16), channel_id=1, source_target_pairs={{0,16},{8,24},{16,0},{24,8},{1,17},{9,25},{17,1},{25,9},{2,18},{10... | collective-permute-start | bytes 3538952 | tf_op jit(solution)/shard_map/ppermute | solution.py:30
  95.5 27.3 %collective-permute-start.24 = (bf16[384,1536]{1,0:T(8,128)(2,1)S(1)}, bf16[384,1536]{1,0:T(8,128)(2,1)S(1)}, u32[]{:S(2)}, u32[]{:S(2)}) collective-permute-start(bf16[384,1536]{1,0:T(8,128)(2,1)S(1)} %pad_maximum_fusion.15), channel_id=1, source_target_pairs={{0,1},{1,0},{2,3},{3,2},{4,5},{5,4},{6,7},{7,6},{8,9},{9,8},{10,11... | collective-permute-start | bytes 3538952 | tf_op jit(solution)/shard_map/ppermute | solution.py:30
  123.1 26.7 %collective-permute-start.25 = (bf16[384,3072]{1,0:T(8,128)(2,1)S(1)}, bf16[384,3072]{1,0:T(8,128)(2,1)S(1)}, u32[]{:S(2)}, u32[]{:S(2)}) collective-permute-start(bf16[384,3072]{1,0:T(8,128)(2,1)S(1)} %pad_maximum_fusion.4), channel_id=1, source_target_pairs={{0,8},{8,0},{16,24},{24,16},{1,9},{9,1},{17,25},{25,17},{2,10},{10... | collective-permute-start | bytes 7077896 | tf_op jit(solution)/shard_map/ppermute | solution.py:30
  124.4 26.9 %collective-permute-start.28 = (bf16[384,3072]{1,0:T(8,128)(2,1)S(1)}, bf16[384,3072]{1,0:T(8,128)(2,1)S(1)}, u32[]{:S(2)}, u32[]{:S(2)}) collective-permute-start(bf16[384,3072]{1,0:T(8,128)(2,1)S(1)} %pad_maximum_fusion.5), channel_id=1, source_target_pairs={{0,8},{8,0},{16,24},{24,16},{1,9},{9,1},{17,25},{25,17},{2,10},{10... | collective-permute-start | bytes 7077896 | tf_op jit(solution)/shard_map/ppermute | solution.py:30
  126.3 21.1 %collective-permute-start.14 = (bf16[64,896]{1,0:T(8,128)(2,1)S(1)}, bf16[64,896]{1,0:T(8,128)(2,1)S(1)}, u32[]{:S(2)}, u32[]{:S(2)}) collective-permute-start(bf16[64,896]{1,0:T(8,128)(2,1)S(1)} %get-tuple-element.35.refs_0_), channel_id=1, source_target_pairs={{0,2},{2,0},{4,6},{6,4},{1,3},{3,1},{5,7},{7,5},{8,10},{10,8},{12,... | collective-permute-start | bytes 344072 | tf_op jit(solution)/shard_map/ppermute | solution.py:30
  165.3 40.7 %collective-permute-start.30 = (bf16[64,768]{1,0:T(8,128)(2,1)S(1)}, bf16[64,768]{1,0:T(8,128)(2,1)S(1)}, u32[]{:S(2)}, u32[]{:S(2)}) collective-permute-start(bf16[64,768]{1,0:T(8,128)(2,1)S(1)} %gmix_body.1.refs_0_), channel_id=1, source_target_pairs={{0,2},{2,0},{4,6},{6,4},{1,3},{3,1},{5,7},{7,5},{8,10},{10,8},{12,... | collective-permute-start | bytes 294920 | tf_op jit(solution)/shard_map/ppermute | solution.py:30
  165.4 40.7 %collective-permute-start.31 = (bf16[64,768]{1,0:T(8,128)(2,1)S(1)}, bf16[64,768]{1,0:T(8,128)(2,1)S(1)}, u32[]{:S(2)}, u32[]{:S(2)}) collective-permute-start(bf16[64,768]{1,0:T(8,128)(2,1)S(1)} %gmix_body.1.refs_0_), channel_id=1, source_target_pairs={{0,4},{2,6},{4,0},{6,2},{1,5},{3,7},{5,1},{7,3},{8,12},{10,14},{12... | collective-permute-start | bytes 294920 | tf_op jit(solution)/shard_map/ppermute | solution.py:30
  167.2 38.9 %collective-permute-start.32 = (bf16[64,768]{1,0:T(8,128)(2,1)S(1)}, bf16[64,768]{1,0:T(8,128)(2,1)}, u32[]{:S(2)}, u32[]{:S(2)}) collective-permute-start(bf16[64,768]{1,0:T(8,128)(2,1)S(1)} %gmix_body.1.refs_0_), channel_id=1, source_target_pairs={{0,6},{2,4},{4,2},{6,0},{1,7},{3,5},{5,3},{7,1},{8,14},{10,12},{12... | collective-permute-start | bytes 294920 | tf_op jit(solution)/shard_map/ppermute | solution.py:30
  198.1 71.2 %collective-permute-start.29 = (bf16[256,768]{1,0:T(8,128)(2,1)}, bf16[256,768]{1,0:T(8,128)(2,1)}, u32[]{:S(2)}, u32[]{:S(2)}) collective-permute-start(bf16[256,768]{1,0:T(8,128)(2,1)} %fusion.20), channel_id=1, source_target_pairs={{0,1},{1,0},{2,3},{3,2},{4,5},{5,4},{6,7},{7,6},{8,9},{9,8},{10,11... | collective-permute-start | bytes 1179656 | tf_op jit(solution)/shard_map/ppermute | solution.py:30
  199.6 100.5 %collective-permute-start.50 = (bf16[384,3072]{1,0:T(8,128)(2,1)}, bf16[384,3072]{1,0:T(8,128)(2,1)}, u32[]{:S(2)}, u32[]{:S(2)}) collective-permute-start(bf16[384,3072]{1,0:T(8,128)(2,1)} %slice.490), channel_id=1, source_target_pairs={{0,8},{8,0},{16,24},{24,16},{1,9},{9,1},{17,25},{25,17},{2,10},{10... | collective-permute-start | bytes 7077896 | tf_op jit(solution)/shard_map/ppermute | solution.py:30
  213.4 24.4 %collective-permute-start.37 = (bf16[16,1536]{1,0:T(8,128)(2,1)S(1)}, bf16[16,1536]{1,0:T(8,128)(2,1)S(1)}, u32[]{:S(2)}, u32[]{:S(2)}) collective-permute-start(bf16[16,1536]{1,0:T(8,128)(2,1)S(1)} %get-tuple-element.155), channel_id=1, source_target_pairs={{0,6},{2,4},{4,2},{6,0},{1,7},{3,5},{5,3},{7,1},{8,14},{10,12},{12... | collective-permute-start | bytes 147464 | tf_op jit(solution)/shard_map/ppermute | solution.py:30
  213.5 24.4 %collective-permute-start.36 = (bf16[16,1536]{1,0:T(8,128)(2,1)S(1)}, bf16[16,1536]{1,0:T(8,128)(2,1)S(1)}, u32[]{:S(2)}, u32[]{:S(2)}) collective-permute-start(bf16[16,1536]{1,0:T(8,128)(2,1)S(1)} %get-tuple-element.156), channel_id=1, source_target_pairs={{0,4},{2,6},{4,0},{6,2},{1,5},{3,7},{5,1},{7,3},{8,12},{10,14},{12... | collective-permute-start | bytes 147464 | tf_op jit(solution)/shard_map/ppermute | solution.py:30
  214.4 24.0 %collective-permute-start.35 = (bf16[16,1536]{1,0:T(8,128)(2,1)S(1)}, bf16[16,1536]{1,0:T(8,128)(2,1)S(1)}, u32[]{:S(2)}, u32[]{:S(2)}) collective-permute-start(bf16[16,1536]{1,0:T(8,128)(2,1)S(1)} %get-tuple-element.154), channel_id=1, source_target_pairs={{0,2},{2,0},{4,6},{6,4},{1,3},{3,1},{5,7},{7,5},{8,10},{10,8},{12,... | collective-permute-start | bytes 147464 | tf_op jit(solution)/shard_map/ppermute | solution.py:30
  237.9 65.8 %collective-permute-start.47 = (bf16[384,3072]{1,0:T(8,128)(2,1)}, bf16[384,3072]{1,0:T(8,128)(2,1)}, u32[]{:S(2)}, u32[]{:S(2)}) collective-permute-start(bf16[384,3072]{1,0:T(8,128)(2,1)} %slice.484), channel_id=1, source_target_pairs={{0,8},{8,0},{16,24},{24,16},{1,9},{9,1},{17,25},{25,17},{2,10},{10... | collective-permute-start | bytes 7077896 | tf_op jit(solution)/shard_map/ppermute | solution.py:30
  237.9 34.9 %collective-permute-start.42 = (bf16[384,1536]{0,1:T(8,128)(2,1)}, bf16[384,1536]{0,1:T(8,128)(2,1)}, u32[]{:S(2)}, u32[]{:S(2)}) collective-permute-start(bf16[384,1536]{0,1:T(8,128)(2,1)} %slice.472), channel_id=1, source_target_pairs={{0,8},{8,0},{16,24},{24,16},{1,9},{9,1},{17,25},{25,17},{2,10},{10... | collective-permute-start | bytes 3538952 | tf_op jit(solution)/shard_map/ppermute | solution.py:30
  303.5 29.2 %collective-permute-start.51 = (bf16[192,3072]{1,0:T(8,128)(2,1)S(1)}, bf16[192,3072]{1,0:T(8,128)(2,1)S(1)}, u32[]{:S(2)}, u32[]{:S(2)}) collective-permute-start(bf16[192,3072]{1,0:T(8,128)(2,1)S(1)} %slice.492), channel_id=1, source_target_pairs={{0,16},{8,24},{16,0},{24,8},{1,17},{9,25},{17,1},{25,9},{2,18},{10... | collective-permute-start | bytes 3538952 | tf_op jit(solution)/shard_map/ppermute | solution.py:30
  306.4 27.4 %collective-permute-start.48 = (bf16[384,1536]{1,0:T(8,128)(2,1)S(1)}, bf16[384,1536]{1,0:T(8,128)(2,1)S(1)}, u32[]{:S(2)}, u32[]{:S(2)}) collective-permute-start(bf16[384,1536]{1,0:T(8,128)(2,1)S(1)} %slice.486), channel_id=1, source_target_pairs={{0,1},{1,0},{2,3},{3,2},{4,5},{5,4},{6,7},{7,6},{8,9},{9,8},{10,11... | collective-permute-start | bytes 3538952 | tf_op jit(solution)/shard_map/ppermute | solution.py:30
  335.5 29.4 %collective-permute-start.45 = (bf16[96,1536]{0,1:T(8,128)(2,1)S(1)}, bf16[96,1536]{0,1:T(8,128)(2,1)S(1)}, u32[]{:S(2)}, u32[]{:S(2)}) collective-permute-start(bf16[96,1536]{0,1:T(8,128)(2,1)S(1)} %pad_maximum_fusion.39), channel_id=1, source_target_pairs={{0,4},{2,6},{4,0},{6,2},{1,5},{3,7},{5,1},{7,3},{8,12},{10,14},{12... | collective-permute-start | bytes 884744 | tf_op jit(solution)/shard_map/ppermute | solution.py:30
  346.8 30.0 %collective-permute-start.53 = (bf16[96,3072]{1,0:T(8,128)(2,1)S(1)}, bf16[96,3072]{1,0:T(8,128)(2,1)S(1)}, u32[]{:S(2)}, u32[]{:S(2)}) collective-permute-start(bf16[96,3072]{1,0:T(8,128)(2,1)S(1)} %pad_maximum_fusion.34), channel_id=1, source_target_pairs={{0,4},{2,6},{4,0},{6,2},{1,5},{3,7},{5,1},{7,3},{8,12},{10,14},{12... | collective-permute-start | bytes 1769480 | tf_op jit(solution)/shard_map/ppermute | solution.py:30
  (118 other events, 1054.7 us)

commit v2 on v1

v2 whole, which is shorter than its diff:
```python
import functools

import jax
import jax.numpy as jnp
from jax import lax
from jax.experimental import pallas as pl
from jax.experimental.pallas import tpu as pltpu
from jax.sharding import PartitionSpec as P

HEAD_DIM = 64
KW = 33
REACH = KW // 2
NEWTON = 6
EPS = 1e-05
SCALE = HEAD_DIM**-0.5
BLOCK = 256
PACK = BLOCK // HEAD_DIM
META = 128
BF = jnp.bfloat16
F32 = jnp.float32
HI = lax.Precision.HIGHEST


def dot(spec, a, b):
    return jnp.einsum(spec, a, b, preferred_element_type=F32)


def hdot(spec, a, b):
    return jnp.einsum(spec, a, b, preferred_element_type=F32, precision=HI)


def swap(a, axis, mask):
    return lax.ppermute(a, axis, [(i, i ^ mask) for i in range(lax.axis_size(axis))])


def swap_both(a, mask):
    nf = lax.axis_size("fsdp")
    return lax.ppermute(a, ("fsdp", "tp"), [(2 * i + j, 2 * (i ^ mask) + (j ^ 1)) for i in range(nf) for j in range(2)])


def add(*terms):
    return sum(t.astype(F32) for t in terms).astype(BF)


def later(value, *after):
    return lax.optimization_barrier((value, after))[0]


def nn(a, b):
    return lax.dot_general(a, b, (((1,), (0,)), ((), ())), preferred_element_type=F32)


def nt(a, b):
    return lax.dot_general(a, b, (((1,), (1,)), ((), ())), preferred_element_type=F32)


def tn(a, b):
    return lax.dot_general(a, b, (((0,), (0,)), ((), ())), preferred_element_type=F32)


def lane_head(rows):
    return lax.broadcasted_iota(jnp.int32, (rows, BLOCK), 1) // HEAD_DIM


def expand(r):
    head = lane_head(HEAD_DIM)
    wide = r.astype(F32)
    return jnp.concatenate([jnp.where(head == i, wide, 0.0) for i in range(PACK)], 0).astype(r.dtype)


def compress(full):
    head = lane_head(HEAD_DIM)
    out = jnp.zeros((HEAD_DIM, BLOCK), F32)
    for i in range(PACK):
        out = jnp.where(head == i, full[i * HEAD_DIM : (i + 1) * HEAD_DIM], out)
    return out


def split(a):
    high = a.astype(BF)
    return high, (a - high.astype(F32)).astype(BF)


def mm3(a, b):
    ah, al = split(a)
    bh, bl = split(b)
    wide = expand(bh)
    return nn(ah, wide) + nn(al, wide) + nn(ah, expand(bl))


def tn3(a, b):
    ah, al = split(a)
    bh, bl = split(b)
    return compress(tn(ah, bh) + tn(al, bh) + tn(ah, bl))


def eye_row():
    row = lax.broadcasted_iota(jnp.int32, (HEAD_DIM, BLOCK), 0)
    lane = lax.broadcasted_iota(jnp.int32, (HEAD_DIM, BLOCK), 1)
    return jnp.where(row == lane % HEAD_DIM, 1.0, 0.0)


def head_total(a):
    head = lane_head(1)
    col = jnp.sum(a, axis=0, keepdims=True)
    out = jnp.zeros_like(col)
    for i in range(PACK):
        one = jnp.sum(jnp.where(head == i, col, 0.0), axis=1, keepdims=True)
        out = jnp.where(head == i, one, out)
    return out


def heads_sum(a):
    parts = a.reshape(PACK, HEAD_DIM, a.shape[1])
    return jnp.broadcast_to(jnp.sum(parts, axis=1, keepdims=True), parts.shape).reshape(a.shape)


def heads_max(a):
    parts = a.reshape(PACK, HEAD_DIM, a.shape[1])
    return jnp.broadcast_to(jnp.max(parts, axis=1, keepdims=True), parts.shape).reshape(a.shape)


def tall(mask):
    return jnp.concatenate([mask] * PACK, 0) > 0.5


def group(g):
    return slice(g * BLOCK, (g + 1) * BLOCK)


def as_row(col, lanes, shift=0, flip=False):
    n = col.shape[0]
    row = lax.broadcasted_iota(jnp.int32, (n, lanes), 0)
    lane = lax.broadcasted_iota(jnp.int32, (n, lanes), 1) - shift
    hit = (row + lane == n - 1) if flip else (row == lane)
    return jnp.sum(jnp.where(hit, col, 0.0), axis=0, keepdims=True)


def rows_at(ref, index, count):
    return ref[pl.ds(pl.multiple_of(index * count, count), count), :]


def call(body, outs, *args, us=2.0, raw_in=(), raw_out=(), far_in=(), far_out=(), smem=(), scratch=(), mem=8, name=None):
    n, m = len(args), len(outs)
    far_in, far_out = list(far_in), list(far_out)

    def space(outside):
        return pltpu.HBM if outside else pltpu.VMEM

    ins = [space(i in raw_in or i in far_in) for i in range(n)]
    res = [space(i in raw_out or i in far_out) for i in range(m)]

    def inner(*refs):
        given, made, extra = list(refs[:n]), list(refs[n : n + m]), refs[n + m :]
        vm_in, extra = extra[: len(far_in)], extra[len(far_in) :]
        vm_out, extra = extra[: len(far_out)], extra[len(far_out) :]
        sem_in, sem_out, rest = extra[0], extra[1], extra[2:]
        loads = [pltpu.make_async_copy(given[i], v, sem_in.at[j]) for j, (i, v) in enumerate(zip(far_in, vm_in))]
        stores = [pltpu.make_async_copy(v, made[i], sem_out.at[j]) for j, (i, v) in enumerate(zip(far_out, vm_out))]
        for c in loads:
            c.start()
        for i, v in zip(far_in, vm_in):
            given[i] = v
        for i, v in zip(far_out, vm_out):
            made[i] = v

        def ready():
            for c in loads:
                c.wait()

        body(ready, *given, *made, *rest)
        for c in stores:
            c.start()
        for c in stores:
            c.wait()

    return pl.pallas_call(
        inner,
        out_shape=[r(*o) for r, o in zip(res, outs)],
        in_specs=[pl.BlockSpec(memory_space=pltpu.SMEM if i in smem else ins[i]) for i in range(n)],
        out_specs=[pl.BlockSpec(memory_space=r) for r in res],
        scratch_shapes=[pltpu.VMEM(args[i].shape, args[i].dtype) for i in far_in]
        + [pltpu.VMEM(*outs[i]) for i in far_out]
        + [pltpu.SemaphoreType.DMA((max(len(far_in), 1),)), pltpu.SemaphoreType.DMA((max(len(far_out), 1),))]
        + list(scratch),
        compiler_params=pltpu.CompilerParams(vmem_limit_bytes=mem << 20),
        cost_estimate=pl.CostEstimate(flops=int(us * 1e7), bytes_accessed=1024, transcendentals=0),
        name=name or body.__name__,
    )(*[a if i in smem else pltpu.with_memory_space_constraint(a, ins[i]) for i, a in enumerate(args)])


def combine(plan, *arrays, near=True, far_in=()):
    shapes = [
        (arrays[parts[0][0][0]][parts[0][0][1]].shape[:-1], [arrays[p[0][0]][p[0][1]].shape[-1] for p in parts]) for parts in plan
    ]
    if not near:
        return [
            jnp.concatenate([add(*[arrays[i][at] for i, at in terms]) for terms in parts], -1) if len(parts) > 1
            else add(*[arrays[i][at] for i, at in parts[0]])
            for parts in plan
        ]

    def sum_body(ready, *refs):
        ready()
        ins, res = refs[: len(arrays)], refs[len(arrays) :]
        for parts, (_, widths), out in zip(plan, shapes, res):
            col = 0
            for terms, width in zip(parts, widths):
                total = sum(ins[i][at].astype(F32) for i, at in terms).astype(BF)
                out[..., col : col + width] = total
                col += width

    return call(sum_body, [(lead + (sum(w),), BF) for lead, w in shapes], *arrays, far_in=far_in, mem=16)


def simple(body):
    def run(ready, *refs):
        ready()
        body(*refs)

    run.__name__ = body.__name__
    return run


def proj_body(ready, x_ref, hb_ref, doc_ref, first_ref, last_ref, *refs):
    parts, refs = refs[:8], refs[8:]
    q_ref, k_ref, v_ref, qkv_hbm, piece_ref, vfirst_ref, vlast_ref, w_hbm, w_ref, sem, sem_w, sem_f = refs
    rows = parts[0].shape[0]
    loads = [
        pltpu.make_async_copy(parts[i], w_ref.at[i // 4, pl.ds((i % 4) * rows, rows)], sem.at[i]) for i in range(8)
    ]
    for c in loads:
        c.start()
    ready()
    T, D = x_ref.shape
    C = D // 2
    x = x_ref[...]
    LL = piece_ref.shape[0]
    seg_len = T // LL
    row = lax.broadcasted_iota(jnp.int32, (LL, T), 0)
    col = lax.broadcasted_iota(jnp.int32, (LL, T), 1)
    mean = jnp.where(col // seg_len == row, 1.0 / seg_len, 0.0).astype(BF)
    store = pltpu.make_async_copy(w_ref, w_hbm, sem_w)
    for c in loads:
        c.wait()
    store.start()
    for side in range(2):
        cols = slice(side * C, (side + 1) * C)
        q = (nn(x, w_ref[side, :, :C]) + hb_ref[0:1, cols]).astype(BF)
        k = nn(x, w_ref[side, :, C : 2 * C]).astype(BF)
        v = (nn(x, w_ref[side, :, 2 * C : 3 * C]) + hb_ref[1:2, cols]).astype(BF)
        q_ref[:, cols] = q
        k_ref[:, cols] = k
        v_ref[:, cols] = v
        vfirst_ref[:, cols] = v[:REACH]
        vlast_ref[:, cols] = v[T - REACH :]
        piece_ref[:, cols] = nn(mean, q).astype(BF)
        piece_ref[:, D + side * C : D + (side + 1) * C] = nn(mean, k).astype(BF)
    piece_ref[:, 2 * D :] = doc_ref[...]
    vfirst_ref[:, D:] = first_ref[...]
    vlast_ref[:, D:] = last_ref[...]
    extra = [pltpu.make_async_copy(r, qkv_hbm.at[i], sem_f.at[i]) for i, r in enumerate((q_ref, k_ref, v_ref))]
    for c in extra:
        c.start()
    for c in extra:
        c.wait()
    store.wait()


def scores_body(n, ready, where_ref, q_ref, k_ref, v_ref, seg_ref, *refs):
    pieces, (ktok_ref, ekey_ref, pack_ref, land_ref, land_far_ref) = refs[:n], refs[n:]
    ready()
    LL = pieces[0].shape[0]
    E = q_ref.shape[1]
    for p in range(n):
        at = pl.multiple_of((where_ref[1] ^ p) * LL, LL)
        land_ref[pl.ds(at, LL), :] = pieces[p][...]
    doc = land_ref[:, 2 * E : 2 * E + 1].astype(F32)
    land_far_ref[...] = land_ref[...]
    allowed = tall((doc == as_row(seg_ref[...], q_ref.shape[0])).astype(F32))
    lane = lax.broadcasted_iota(jnp.int32, (HEAD_DIM, META), 1)
    stats = jnp.zeros((HEAD_DIM, META), F32)
    heads = E // HEAD_DIM
    for g in range(E // BLOCK):
        s = group(g)
        lq, lk = land_ref[:, s], land_ref[:, E + g * BLOCK : E + (g + 1) * BLOCK]
        z = nt(expand(lk), q_ref[:, s]) * SCALE
        z = jnp.where(allowed, z, -1e30)
        e = jnp.where(allowed, jnp.exp(z - heads_max(z)), 0.0)
        ktok_ref[s, :] = (e / heads_sum(e)).astype(BF)
        z = nt(expand(lq), k_ref[:, s]) * SCALE
        z = jnp.where(allowed, z, -1e30)
        top = jnp.max(z, axis=1, keepdims=True)
        e = jnp.where(allowed, jnp.exp(z - top), 0.0)
        total = jnp.sum(e, axis=1, keepdims=True)
        low = e.astype(BF)
        ekey_ref[s, :] = low
        pack_ref[:, s] = compress(nn(low, v_ref[:, s])).astype(BF)
        for i in range(PACK):
            h = g * PACK + i
            rows = slice(i * HEAD_DIM, (i + 1) * HEAD_DIM)
            stats = jnp.where(lane == h, top[rows], stats)
            stats = jnp.where(lane == heads + h, total[rows], stats)
    first = stats.astype(BF).astype(F32)
    second = (stats - first).astype(BF).astype(F32)
    third = stats - first - second
    pack_ref[:, E:] = (first + pltpu.roll(second, 2 * heads, 1) + pltpu.roll(third, 4 * heads, 1)).astype(BF)


def newton_body(land_ref, kt_ref, mixer_ref, p_ref, w_ref, pi_ref):
    E = kt_ref.shape[1]
    eye = eye_row()
    doc = land_ref[:, 2 * E : 2 * E + 1].astype(F32)
    allowed = jnp.concatenate([(doc == as_row(doc, HEAD_DIM)).astype(F32)] * PACK, 1) > 0.5
    groups = [group(g) for g in range(E // BLOCK)]
    kts, invs, ps, pis = [], [], [], []
    for s in groups:
        lq, lk = land_ref[:, s], land_ref[:, E + s.start : E + s.stop]
        z = nt(lk, expand(lq)) * SCALE
        z = jnp.where(allowed, z, -1e30)
        e = jnp.where(allowed, jnp.exp(z - jnp.max(z, axis=0, keepdims=True)), 0.0)
        kt = e / jnp.sum(e, axis=0, keepdims=True)
        kts.append(kt)
        invs.append(1.0 / head_total(kt * kt))
        kt_ref[:, s] = kt
    ps = [tn3(kt, kt) * inv for kt, inv in zip(kts, invs)]
    for step in range(NEWTON):
        for s, p in zip(groups, ps):
            p_ref[step, :, s] = p
        p2s = [mm3(p, p) for p in ps]
        ws = [0.25 * (13.0 * eye - 15.0 * p + mm3(p2, 7.0 * eye - p)) for p, p2 in zip(ps, p2s)]
        if step < NEWTON - 1:
            ps = [mm3(p, w) for p, w in zip(ps, ws)]
        pis = [mm3(pi, w) for pi, w in zip(pis, ws)] if step else ws
        for s, w, pi in zip(groups, ws, pis):
            w_ref[step, :, s] = w
            pi_ref[step, :, s] = pi
    for s, kt, pi, inv in zip(groups, kts, pis, invs):
        mixer_ref[:, s] = mm3(kt, pi) * inv


def newton_back_body(land_ref, kt_ref, p_ref, w_ref, pi_ref, mixer_ref, gmix_ref, lval_ref, where_ref, own_ref, full_ref):
    E = kt_ref.shape[1]
    groups = [group(g) for g in range(E // BLOCK)]
    many = range(len(groups))
    kts = [kt_ref[:, s] for s in groups]
    invs = [1.0 / head_total(kt * kt) for kt in kts]
    grads = []
    for s in groups:
        gh, gl = split(gmix_ref[:, s])
        vh, vl = split(lval_ref[:, s])
        wide = expand(vh)
        grads.append(nt(gh, wide) + nt(gl, wide) + nt(gh, expand(vl)))
    d_pis = [tn3(kts[i], grads[i]) * invs[i] for i in many]
    d_kts = [mm3(grads[i], pi_ref[NEWTON - 1, :, groups[i]]) * invs[i] for i in many]
    d_cs = [-head_total(grads[i] * mixer_ref[:, groups[i]]) * invs[i] for i in many]
    d_ps = None
    for step in reversed(range(NEWTON)):
        ps = [p_ref[step, :, s] for s in groups]
        ws = [w_ref[step, :, s] for s in groups]
        d_ws = [mm3(pi_ref[step - 1, :, groups[i]], d_pis[i]) for i in many] if step else d_pis
        if d_ps is not None:
            d_ws = [d_ws[i] + mm3(ps[i], d_ps[i]) for i in many]
            d_ps = [mm3(d_ps[i], ws[i]) for i in many]
        if step:
            d_pis = [mm3(d_pis[i], ws[i]) for i in many]
        ones = [mm3(ps[i], d_ws[i]) for i in many]
        twos = [ones[i] + mm3(d_ws[i], ps[i]) for i in many]
        more = [
            0.25 * (7.0 * twos[i] - 15.0 * d_ws[i] - mm3(ps[i], ones[i]) - mm3(twos[i], ps[i])) for i in many
        ]
        d_ps = more if d_ps is None else [d_ps[i] + more[i] for i in many]
    for i in many:
        s, kt, inv = groups[i], kts[i], invs[i]
        lq, lk = land_ref[:, s], land_ref[:, E + s.start : E + s.stop]
        d_c = d_cs[i] - head_total(d_ps[i] * p_ref[0, :, s]) * inv
        kh, kl = split(kt)
        sh, sl = split(d_ps[i] * inv)
        wide = expand(sh)
        thin = expand(sl)
        d_kt = d_kts[i] + nn(kh, wide) + nn(kl, wide) + nn(kh, thin) + nt(kh, wide) + nt(kl, wide) + nt(kh, thin)
        d_kt = d_kt + 2.0 * d_c * kt
        dz = kt * (d_kt - jnp.sum(kt * d_kt, axis=0, keepdims=True)) * SCALE
        zh, zl = split(dz)
        wide = expand(lq)
        full_ref[:, E + s.start : E + s.stop] = nn(zh, wide) + nn(zl, wide)
        full_ref[:, s] = compress(tn(zh, lk) + tn(zl, lk))
    own_ref[...] = rows_at(full_ref, where_ref[1], own_ref.shape[0])


def mix_part(packs, mixer_ref, ktok_ref, conv_ref, mixing_ref, lval_ref, scale_ref, mixed_ref):
    E = mixer_ref.shape[1]
    heads = E // HEAD_DIM
    stats = []
    for p in packs:
        tile = p[:, E:].astype(F32)
        stats.append(tile + pltpu.roll(tile, 128 - 2 * heads, 1) + pltpu.roll(tile, 128 - 4 * heads, 1))
    top = stats[0]
    for t in stats[1:]:
        top = jnp.maximum(top, t)
    lane = lax.broadcasted_iota(jnp.int32, (HEAD_DIM, 128), 1)
    weights = [jnp.where(lane < heads, jnp.exp(jnp.minimum(t - top, 0.0)), 0.0) for t in stats]
    total = sum(w * pltpu.roll(t, 128 - heads, 1) for w, t in zip(weights, stats))
    total = jnp.where(lane < heads, total, 1.0)
    weights = [w / total for w in weights]
    scale_ref[...] = weights[0]
    head = lane_head(HEAD_DIM)
    for g in range(E // BLOCK):
        s = group(g)
        lval = jnp.zeros((HEAD_DIM, BLOCK), F32)
        for w, p in zip(weights, packs):
            spread = jnp.zeros((HEAD_DIM, BLOCK), F32)
            for i in range(PACK):
                h = g * PACK + i
                spread = jnp.where(head == i, w[:, h : h + 1], spread)
            lval = lval + spread * p[:, s].astype(F32)
        lval_ref[:, s] = lval
        mixing = mm3(mixer_ref[:, s], lval)
        mixing_ref[:, s] = mixing
        mh, ml = split(mixing)
        tok = ktok_ref[s, :]
        mixed_ref[:, s] = (tn(tok, expand(mh)) + tn(tok, expand(ml)) + conv_ref[:, s].astype(F32)).astype(BF)


def norm_part(r):
    center = r - jnp.mean(r, axis=1, keepdims=True)
    inv = lax.rsqrt(jnp.mean(center * center, axis=1, keepdims=True) + EPS)
    return center * inv, inv


def norm_back(e, n, inv, gain):
    eg = e * gain
    return (eg - jnp.mean(eg, axis=1, keepdims=True) - n * jnp.mean(eg * n, axis=1, keepdims=True)) * inv


def pair_pick(first, second):
    lane = lax.broadcasted_iota(jnp.int32, first.shape, 1)
    return jnp.where(lane < HEAD_DIM, first, second)


def band_apply(row, band, edge, a_ref, rim_ref, cols):
    T = a_ref.shape[0]
    wide = pltpu.roll(jnp.broadcast_to(row, (T, T)), 0, 1, stride=1, stride_axis=0)
    wide = jnp.where(band, wide, 0.0).astype(BF)
    short = jnp.broadcast_to(row, (REACH, T))
    rims = jnp.concatenate(
        [
            pltpu.roll(short, REACH, 1, stride=1, stride_axis=0),
            pltpu.roll(short, 0, 1, stride=1, stride_axis=0),
        ],
        0,
    )[:, :128]
    rims = jnp.where(edge, rims, 0.0).astype(BF)
    return nn(wide, a_ref[:, cols]), nn(rims, rim_ref[:, cols])


def conv_pair(rows_ref, band, edge, a_ref, rim_ref, out_ref, j):
    T = a_ref.shape[0]
    cols = slice(j * 128, (j + 1) * 128)
    one, one_rim = band_apply(rows_ref[2 * j : 2 * j + 1, :], band, edge, a_ref, rim_ref, cols)
    two, two_rim = band_apply(rows_ref[2 * j + 1 : 2 * j + 2, :], band, edge, a_ref, rim_ref, cols)
    both, rim = pair_pick(one, two), pair_pick(one_rim, two_rim)
    out_ref[:REACH, cols] = (both[:REACH] + rim[:REACH]).astype(BF)
    out_ref[REACH : T - REACH, cols] = both[REACH : T - REACH].astype(BF)
    out_ref[T - REACH :, cols] = (both[T - REACH :] + rim[REACH:]).astype(BF)


def band_of(col_ref, flip):
    T = col_ref.shape[0]
    a = lax.broadcasted_iota(jnp.int32, (T, T), 0)
    b = lax.broadcasted_iota(jnp.int32, (T, T), 1)
    gap = (T - 1 - b - a) if flip else (b - a)
    return (jnp.abs(gap) <= REACH) & (as_row(col_ref[...], T, 0, flip) == col_ref[...])


def edge_of(col_ref, before, after, flip):
    T = col_ref.shape[0]
    row = lax.broadcasted_iota(jnp.int32, (REACH, META), 0)
    lane = lax.broadcasted_iota(jnp.int32, (REACH, META), 1)
    shift = 0 if flip else REACH
    i = (REACH - 1 - lane) if flip else lane
    j = (REACH - 1 - lane) if flip else lane - REACH
    low = (i >= row) & (i < REACH) & (as_row(before, META, 0, flip) == col_ref[:REACH] + 1.0)
    high = (j <= row) & (j >= 0) & (as_row(after, META, shift, flip) == col_ref[T - REACH :] + 1.0)
    return jnp.concatenate([low.astype(F32), high.astype(F32)], 0) > 0.5


def rim_of(before_ref, after_ref, E):
    return jnp.concatenate([before_ref[:, :E], after_ref[:, :E], jnp.zeros((META - 2 * REACH, E), BF)], 0)


def conv_body(rows_ref, seg_col_ref, v_ref, before_ref, after_ref, out_ref):
    E = v_ref.shape[1]
    band = band_of(seg_col_ref, False)
    edge = edge_of(seg_col_ref, before_ref[:, E : E + 1].astype(F32), after_ref[:, E : E + 1].astype(F32), False)
    rim = rim_of(before_ref, after_ref, E)
    for j in range(E // 128):
        conv_pair(rows_ref, band, edge, v_ref, rim, out_ref, j)


def conv_back_body(
    rows_ref, seg_col_ref, g_ref, g_before_ref, g_after_ref, qkv_ref, before_ref, after_ref, out_ref, tap_ref
):
    T, E = g_ref.shape
    v_ref = qkv_ref.at[2]
    seg_before, seg_after = before_ref[:, E : E + 1].astype(F32), after_ref[:, E : E + 1].astype(F32)
    band = band_of(seg_col_ref, False)
    edge = edge_of(seg_col_ref, seg_before, seg_after, False)
    band_rev = band_of(seg_col_ref, True)
    edge_rev = edge_of(seg_col_ref, seg_before, seg_after, True)
    g_rim = rim_of(g_before_ref, g_after_ref, E)
    v_rim = rim_of(before_ref, after_ref, E)
    a = lax.broadcasted_iota(jnp.int32, (T, T), 0)
    b = lax.broadcasted_iota(jnp.int32, (T, T), 1)
    flip = jnp.where(a + b == T - 1, 1.0, 0.0).astype(BF)
    a = lax.broadcasted_iota(jnp.int32, (META, META), 0)
    b = lax.broadcasted_iota(jnp.int32, (META, META), 1)
    flip_before = jnp.where(a + b == REACH - 1, 1.0, 0.0).astype(BF)
    flip_after = jnp.where((a + b == 2 * REACH - 1) & (a < REACH), 1.0, 0.0).astype(BF)
    for j in range(E // 128):
        cols = slice(j * 128, (j + 1) * 128)
        conv_pair(rows_ref, band, edge, g_ref, g_rim, out_ref, j)
        v_rev = nn(flip, v_ref[:, cols]).astype(BF)
        before = nn(flip_before, v_rim[:, cols]).astype(BF)
        after = nn(flip_after, v_rim[:, cols]).astype(BF)
        g = g_ref[:, cols].astype(F32)
        lane = lax.broadcasted_iota(jnp.int32, g.shape, 1)
        for i in range(2):
            mine = jnp.where((lane < HEAD_DIM) == (i == 0), g, 0.0).astype(BF)
            h = 2 * j + i
            cross = jnp.where(band_rev, nt(mine, v_rev), 0.0)
            cross = pltpu.roll(cross, 0, 1, stride=1, stride_axis=0)
            tap_ref[h : h + 1, :T] = jnp.sum(cross, axis=0, keepdims=True)
            low = jnp.where(edge_rev[:REACH], nt(mine[:REACH], before), 0.0)
            low = pltpu.roll(low, 0, 1, stride=1, stride_axis=0)
            tap_ref[h : h + 1, T : T + META] = jnp.sum(low, axis=0, keepdims=True)
            high = jnp.where(edge_rev[REACH:], nt(mine[T - REACH :], after), 0.0)
            high = pltpu.roll(high, 0, 1, stride=1, stride_axis=0)
            tap_ref[h : h + 1, T + META :] = jnp.sum(high, axis=0, keepdims=True)


def piece_at(where_ref, p, row_bits, nc):
    f, c = where_ref[0], where_ref[1]
    for i, (axis, mask) in enumerate(row_bits):
        if p >> i & 1:
            if axis == "fsdp":
                f = f ^ mask
            else:
                c = c ^ mask
    return f * nc + c


def mid_body(n, pieces, row_bits, nc, ready, where_ref, *refs):
    packs, refs = refs[:n], refs[n:]
    mixer_ref, ktok_ref, conv_ref, land_ref, x_ref, cot_ref, perm_ref, vec_ref, fb_ref, qkv_hbm, w_hbm, ud_hbm = refs[:12]
    refs = refs[12:]
    gq_ref, lk_ref, lval_ref, scale_ref, mixed_ref, y_ref, gm_ref, gfirst_ref, glast_ref, gmix_ref, first_ref, gb_ref, sums_ref, fbg_ref = refs[:14]
    ku_ref, su_ref, kd_ref, sd_ref = refs[14:18]
    wo, wu, wd, act_ref, dg_ref, mixing_ref, q_ref, sem_in, sem_o = refs[18:]
    T, D = x_ref.shape
    half = D // 2
    FL = wu.shape[2]
    R = D // pieces
    loads = []
    for side in range(2):
        ups, downs = [], []
        for p in range(pieces):
            if pieces > 1:
                at, half_at = piece_at(where_ref, p, row_bits, nc), where_ref[2] ^ side
            else:
                at, half_at = 0, side
            rows = pl.ds(p * R, R)
            k = side * pieces + p
            ups.append(pltpu.make_async_copy(ud_hbm.at[at, half_at, :, pl.ds(0, FL)], wu.at[side, rows], sem_in.at[0, k]))
            downs.append(pltpu.make_async_copy(ud_hbm.at[at, half_at, :, pl.ds(FL, FL)], wd.at[side, rows], sem_in.at[1, k]))
        loads.append((ups, downs))
    load_o = pltpu.make_async_copy(w_hbm.at[:, :, pl.ds(3 * half, half)], wo, sem_o.at[0])
    load_q = pltpu.make_async_copy(qkv_hbm.at[pl.ds(0, 1)], q_ref, sem_o.at[1])
    load_o.start()
    load_q.start()
    for ups, downs in loads:
        for c in ups + downs:
            c.start()
    ready()
    mix_part(packs, mixer_ref, ktok_ref, conv_ref, mixing_ref, lval_ref, scale_ref, mixed_ref)
    gain0, gain1 = vec_ref[0:1], vec_ref[1:2]
    mixed = mixed_ref[...]
    load_o.wait()
    branch = nt(mixed[:, :half], wo[0]) + nt(mixed[:, half:], wo[1])
    n1, inv1 = norm_part(x_ref[...].astype(F32) + branch + vec_ref[4:5])
    hidden = n1 * gain0 + vec_ref[2:3]
    low = hidden.astype(BF)
    step = 512
    ffn = jnp.zeros((T, D), F32)
    cubic, lead = 0.044715, 0.7978845608028654
    for side in range(2):
        for c in loads[side][0] + loads[side][1]:
            c.wait()
        for j in range(FL // step):
            cols = slice(j * step, (j + 1) * step)
            at = slice(side * FL + j * step, side * FL + (j + 1) * step)
            u = nn(low, wu[side, :, cols]) + fb_ref[:, at]
            sq = u * u
            t = jnp.tanh(lead * u * (1.0 + cubic * sq))
            act = (0.5 * u * (1.0 + t)).astype(BF)
            dg_ref[:, at] = 0.5 * (1.0 + t) + 0.5 * u * (1.0 - t * t) * lead * (1.0 + 3.0 * cubic * sq)
            act_ref[:, at] = act
            ffn = ffn + nt(act, wd[side, :, cols])
    n2, inv2 = norm_part(hidden + ffn + vec_ref[5:6])
    y_ref[...] = nt((n2 * gain1 + vec_ref[3:4]).astype(BF), perm_ref[...]).astype(BF)
    cot = cot_ref[...].astype(F32)
    second = norm_back(cot, n2, inv2, gain1)
    sums_ref[1:2] = jnp.sum(cot * n2, axis=0, keepdims=True)
    sums_ref[3:4] = jnp.sum(cot, axis=0, keepdims=True)
    gf = second.astype(BF)
    sums_ref[5:6] = jnp.sum(gf.astype(F32), axis=0, keepdims=True)
    gt = gf.astype(F32).T.astype(BF)
    ht = low.astype(F32).T.astype(BF)
    gh = second
    for side in range(2):
        for j in range(FL // step):
            cols = slice(j * step, (j + 1) * step)
            at = slice(side * FL + j * step, side * FL + (j + 1) * step)
            gu = (nn(gf, wd[side, :, cols]) * dg_ref[:, at]).astype(BF)
            fbg_ref[:, at] = jnp.sum(gu.astype(F32), axis=0, keepdims=True)
            ku_ref[side, :, cols] = nn(ht[:half], gu).astype(BF)
            su_ref[side, :, cols] = nn(ht[half:], gu).astype(BF)
            gh = gh + nt(gu, wu[side, :, cols])
            kd_ref[side, :, cols] = nn(gt[:half], act_ref[:, at]).astype(BF)
            sd_ref[side, :, cols] = nn(gt[half:], act_ref[:, at]).astype(BF)
    first = norm_back(gh, n1, inv1, gain0)
    sums_ref[0:1] = jnp.sum(gh * n1, axis=0, keepdims=True)
    sums_ref[2:3] = jnp.sum(gh, axis=0, keepdims=True)
    first_ref[...] = first
    low = first.astype(BF)
    gb_ref[...] = low
    sums_ref[4:5] = jnp.sum(low.astype(F32), axis=0, keepdims=True)
    sums_ref[6:8] = jnp.zeros((2, D), F32)
    for side in range(2):
        gm = nn(low, wo[side]).astype(BF)
        cols = slice(side * half, (side + 1) * half)
        gm_ref[:, cols] = gm
        gfirst_ref[:, cols] = gm[:REACH]
        glast_ref[:, cols] = gm[T - REACH :]
    load_q.wait()
    for g in range(D // BLOCK):
        s = group(g)
        gm = gm_ref[:, s]
        gmix_ref[:, s] = compress(nn(ktok_ref[s, :], gm)).astype(BF)
        mh, ml = split(mixing_ref[:, s])
        gk = nt(expand(mh), gm) + nt(expand(ml), gm)
        tok = ktok_ref[s, :].astype(F32)
        gz = (tok * (gk - heads_sum(tok * gk)) * SCALE).astype(BF)
        gq_ref[:, s] = tn(gz, expand(land_ref[:, D + s.start : D + s.stop])).astype(BF)
        lk_ref[:, s] = compress(nn(gz, q_ref[0, :, s]))


def key_back_body(n, ready, where_ref, *refs):
    gmixes, refs = refs[:n], refs[n:]
    mixer_ref, lval_ref, ekey_ref, scale_ref, qkv_ref, land_ref, lk_ref = refs[:7]
    gmix_ref, gv_ref, gk_ref, own_ref = refs[7:11]
    sends, full_ref = refs[11:-1], refs[-1]
    k_ref, v_ref = qkv_ref.at[1], qkv_ref.at[2]
    ready()
    E = v_ref.shape[1]
    for g in range(E // BLOCK):
        s = group(g)
        gmix = gmixes[0][:, s].astype(F32)
        for other in gmixes[1:]:
            gmix = gmix + other[:, s].astype(F32)
        gmix_ref[:, s] = gmix
        lval = lval_ref[:, s]
        glval = tn3(mixer_ref[:, s], gmix)
        gh, gl = split(glval)
        wide = expand(gh)
        v = v_ref[:, s]
        gkk = nt(wide, v) + nt(expand(gl), v)
        center = jnp.sum(expand(glval * lval), axis=1, keepdims=True)
        scale = jnp.concatenate([scale_ref[:, g * PACK + i : g * PACK + i + 1] for i in range(PACK)], 0)
        kk = ekey_ref[s, :].astype(F32) * scale
        gz = (kk * (gkk - center) * SCALE).astype(BF)
        gv_ref[:, s] = tn(kk.astype(BF), wide).astype(BF)
        gk_ref[:, s] = tn(gz, expand(land_ref[:, s])).astype(BF)
        full_ref[:, s] = compress(nn(gz, k_ref[:, s]))
    full_ref[:, E:] = lk_ref[...]
    LL = own_ref.shape[0]
    own_ref[...] = rows_at(full_ref, where_ref[1], LL)
    for p, ref in enumerate(sends):
        ref[...] = rows_at(full_ref, where_ref[1] ^ (p + 1), LL).astype(BF)


def grad_body(n, ready, *refs):
    owns, refs = refs[: n + 1], refs[n + 1 :]
    gqt_ref, gkt_ref, gvk_ref, gvc_ref, x_ref, gb_ref, mixed_ref = refs[:7]
    gq_ref, gk_ref, gv_ref, hbg_ref = refs[7:11]
    outs = refs[11:15]
    ready()
    T, D = x_ref.shape
    half = D // 2
    own = owns[0][...]
    for other in owns[1:]:
        own = own + other[...].astype(F32)
    LL = own.shape[0]
    seg_len = T // LL
    own = own * (1.0 / seg_len)
    spread = jnp.broadcast_to(own[:, None, :], (LL, seg_len, 2 * D)).reshape(T, 2 * D)
    gq = (gqt_ref[...].astype(F32) + spread[:, :D]).astype(BF)
    gk = (gkt_ref[...].astype(F32) + spread[:, D:]).astype(BF)
    gv = (gvk_ref[...].astype(F32) + gvc_ref[...].astype(F32)).astype(BF)
    gv_ref[...] = gv
    gq_ref[...] = gq
    gk_ref[...] = gk
    hbg_ref[0:1] = jnp.sum(gq.astype(F32), axis=0, keepdims=True)
    hbg_ref[1:2] = jnp.sum(gv.astype(F32), axis=0, keepdims=True)
    xt = x_ref[...].astype(F32).T.astype(BF)
    gt = gb_ref[...].astype(F32).T.astype(BF)
    mixed = mixed_ref[...]
    for side in range(2):
        cols = slice(side * half, (side + 1) * half)
        for r in range(2):
            rows = slice(r * half, (r + 1) * half)
            outs[r][side, :, :half] = nn(xt[rows], gq[:, cols]).astype(BF)
            outs[r][side, :, half:] = nn(xt[rows], gk[:, cols]).astype(BF)
            outs[2 + r][side, :, :half] = nn(xt[rows], gv[:, cols]).astype(BF)
            outs[2 + r][side, :, half:] = nn(gt[rows], mixed[:, cols]).astype(BF)


def input_grad_body(gq_ref, gk_ref, gv_ref, first_ref, perm_ref, w_ref, out_ref):
    half = first_ref.shape[1] // 2
    total = first_ref[...]
    for side in range(2):
        cols = slice(side * half, (side + 1) * half)
        total = total + nt(gq_ref[:, cols], w_ref[side, :, :half])
        total = total + nt(gk_ref[:, cols], w_ref[side, :, half : 2 * half])
        total = total + nt(gv_ref[:, cols], w_ref[side, :, 2 * half : 3 * half])
    out_ref[...] = nt(total.astype(BF), perm_ref[...]).astype(BF)


def back_body(n, ready, *refs):
    first, second, rest = refs[:n], refs[n : n + 8], refs[n + 8 :]
    ready()
    conv_back_body(*second, rest[1], rest[2])
    newton_back_body(*first, rest[0], rest[3])


def small_body(rows, ready, tap_ref, hbg_ref, fbg_ref, sums_ref, perm_ref, out_ref):
    ready()
    heads, width = tap_ref.shape
    T = width - 2 * META
    D = sums_ref.shape[1]
    top = rows - 7 * D // META - fbg_ref.shape[1] // 2 // META
    t = lax.broadcasted_iota(jnp.int32, (top, T), 0)
    lane = lax.broadcasted_iota(jnp.int32, (top, T), 1)
    main = ((lane + t - (REACH - 1)) % T == 0) & (t < KW)
    t = lax.broadcasted_iota(jnp.int32, (top, META), 0)
    lane = lax.broadcasted_iota(jnp.int32, (top, META), 1)
    before = (lane + t == REACH - 1) & (t < REACH)
    after = (lane + t == 3 * REACH - 1) & (t < KW)
    out = [jnp.zeros((top, META), F32), jnp.zeros((top, META), F32)]
    half = heads // 2
    for h in range(heads):
        row = tap_ref[h : h + 1, :]
        col = jnp.sum(jnp.where(main, row[:, :T], 0.0), axis=1, keepdims=True)
        col = col + jnp.sum(jnp.where(before, row[:, T : T + META], 0.0), axis=1, keepdims=True)
        col = col + jnp.sum(jnp.where(after, row[:, T + META :], 0.0), axis=1, keepdims=True)
        out[h // half] = jnp.where(lane == h % half, col, out[h // half])
    first = sums_ref[...].astype(BF)
    rest = sums_ref[...] - first.astype(F32)
    second = rest.astype(BF)
    third = (rest - second.astype(F32)).astype(BF)
    perm = perm_ref[...]
    sums = nt(first, perm) + nt(second, perm) + nt(third, perm)
    FL = fbg_ref.shape[1] // 2
    for side in range(2):
        ref = out_ref.at[side]
        ref[:top, :] = out[side]
        at = top
        for i in range(2):
            for j in range(D // 2 // META):
                col = side * (D // 2) + j * META
                ref[at : at + 1, :] = hbg_ref[i : i + 1, col : col + META]
                at += 1
        for j in range(FL // META):
            ref[at : at + 1, :] = fbg_ref[:, side * FL + j * META : side * FL + (j + 1) * META]
            at += 1
        for i in range(6):
            for j in range(D // META):
                ref[at : at + 1, :] = sums[i : i + 1, j * META : (j + 1) * META]
                at += 1


def small_out_body(a_ref, b_ref, c_ref, d_ref, conv_ref, hb_ref, fb_ref, gains_ref, offsets_ref):
    total = (a_ref[0] + b_ref[...]) + (c_ref[...] + d_ref[...])
    rows = total.shape[0]
    D = gains_ref.shape[1]
    FL = fb_ref.shape[1]
    at = rows - 7 * D // META - FL // META
    conv_ref[...] = total[:KW, : conv_ref.shape[1]]
    for i in range(2):
        for j in range(D // 2 // META):
            hb_ref[i : i + 1, j * META : (j + 1) * META] = total[at : at + 1]
            at += 1
    for j in range(FL // META):
        fb_ref[:, j * META : (j + 1) * META] = total[at : at + 1]
        at += 1
    for i in range(6):
        ref, r = (gains_ref, i) if i < 2 else (offsets_ref, i - 2)
        for j in range(D // META):
            ref[r : r + 1, j * META : (j + 1) * META] = total[at : at + 1]
            at += 1


def local(x_in, out_cot, seg_ids, land_doc, w_qkv, w_out, w_up, w_down, conv_taps, head_bias, ffn_bias, gains, offsets):
    nf, nc, nt_ = lax.axis_size("fsdp"), lax.axis_size("ctx"), lax.axis_size("tp")
    f_i, c_i, t_i = lax.axis_index("fsdp"), lax.axis_index("ctx"), lax.axis_index("tp")
    assert nt_ == 2 and x_in.shape[0] == 2
    ctx_bits = [("ctx", 1 << b) for b in range(nc.bit_length() - 1)]
    chip_bits = [("fsdp", 1 << b) for b in range(1, nf.bit_length() - 1)]
    core_bit = ("fsdp", 1)
    row_bits = ctx_bits + chip_bits + [core_bit]
    T, D = x_in.shape[1:]
    R = w_qkv.shape[0]
    C = w_qkv.shape[2]
    E = 2 * C
    FL = w_up.shape[1]
    HL = C // HEAD_DIM
    H = 2 * HL
    LL = land_doc.shape[1]
    L = LL * nc
    where = jnp.stack([f_i, c_i, t_i]).astype(jnp.int32)

    def along_ctx(own):
        return [own] + [swap(own, "ctx", p) for p in range(1, nc)]

    ud = lax.all_gather(jnp.concatenate([w_up, w_down], axis=1), ("fsdp", "ctx", "tp"), axis=0, tiled=True)
    ud = ud.reshape(nf * nc, 2, R, 2 * FL)

    zq = along_ctx(jnp.concatenate([w_qkv.reshape(R, 3 * C), w_out], axis=1))
    x_in, out_cot = later((x_in, out_cot), zq[0])

    q_pos = jnp.arange(D, dtype=jnp.int32)
    piece, inner = q_pos // R, q_pos % R
    mf = jnp.zeros_like(piece)
    mc = jnp.zeros_like(piece)
    for i, (axis, mask) in enumerate(row_bits):
        bit = ((piece >> i) & 1) * mask
        if axis == "fsdp":
            mf = mf ^ bit
        else:
            mc = mc ^ bit
    true_piece = (f_i ^ mf) * nc + (c_i ^ mc)
    perm = (jnp.arange(D, dtype=jnp.int32)[:, None] == (true_piece * R + inner)[None, :]).astype(BF)
    aligned = R % 16 == 0
    if not aligned:
        order = true_piece[::R]
        sides = jnp.stack([t_i, 1 - t_i])
        ud = ud[order][:, sides].transpose(1, 0, 2, 3).reshape(1, 2, D, 2 * FL)

    def pick(a):
        return lax.dynamic_index_in_dim(a, t_i, 0, False)

    x = dot("td,dq->tq", pick(x_in), perm).astype(BF)
    cot = dot("td,dq->tq", pick(out_cot), perm).astype(BF)

    own = jnp.concatenate(zq, 0)
    for bit in chip_bits[:-1]:
        own = jnp.concatenate([own, swap(own, *bit)], 0)
    last_bit = chip_bits[-1]
    plane = [own, swap(own, *last_bit), swap(own, "tp", 1), swap_both(own, last_bit[1])]

    seg_ids, land_doc, conv_taps, head_bias, ffn_bias = later((seg_ids, land_doc, conv_taps, head_bias, ffn_bias), zq[0])
    seg = pick(seg_ids).astype(F32)
    doc = pick(land_doc).astype(F32)
    seg_col = seg[:, None]

    def meta(col):
        return jnp.where(jnp.arange(META)[None, :] == 0, col[:, None], 0.0).astype(BF)

    par = jnp.concatenate([conv_taps.reshape(-1), head_bias.reshape(-1), ffn_bias.reshape(-1)])
    par2 = jnp.stack([par, swap(par, "tp", 1)])
    taps = par2[:, : KW * HL].reshape(2, KW, HL).transpose(0, 2, 1).reshape(H, KW)
    hb = par2[:, KW * HL : KW * HL + 2 * C].reshape(2, 2, C).transpose(1, 0, 2).reshape(2, 2 * C)
    fb = par2[:, KW * HL + 2 * C :].reshape(1, 2 * FL)
    vec = hdot("vd,dq->vq", jnp.concatenate([gains, offsets], 0), perm.astype(F32))
    gap = jnp.zeros((H, T - KW), F32)
    taps_rev = taps[:, ::-1]
    row_fwd = jnp.concatenate([taps[:, REACH:], gap, taps[:, :REACH]], 1)
    row_back = jnp.concatenate([taps_rev[:, REACH:], gap, taps_rev[:, :REACH]], 1)

    mine, other = plane[:2], plane[2:]
    parts = mine + [swap(a, *core_bit) for a in mine] + other + [swap(a, *core_bit) for a in other]
    parts = later(parts, hb, fb, vec, row_fwd, row_back, cot)
    q, k, v, qkv, piece0, vfirst, vlast, w_full = call(
        proj_body,
        [((T, E), BF)] * 3 + [((3, T, E), BF), ((LL, 2 * E + META), BF)] + [((REACH, E + META), BF)] * 2 + [((2, D, 4 * C), BF)],
        x, hb, meta(doc), meta(seg[:REACH] + 1.0), meta(seg[T - REACH :] + 1.0), *parts,
        raw_in=range(5, 13),
        raw_out=(3, 7),
        scratch=[pltpu.VMEM((2, D, 4 * C), BF), pltpu.SemaphoreType.DMA((8,)), pltpu.SemaphoreType.DMA, pltpu.SemaphoreType.DMA((3,))],
        mem=14,
    )

    up = [(i, i + 1) for i in range(nc - 1)]
    down = [(i + 1, i) for i in range(nc - 1)]
    pieces = along_ctx(piece0)
    ktok, ekey, pack, land, land_far = call(
        functools.partial(scores_body, nc),
        [((E, T), BF), ((E, T), BF), ((L, E + META), BF), ((L, 2 * E + META), BF), ((L, 2 * E + META), BF)],
        where, q, k, v, seg_col, *pieces, smem=(0,), far_out=(0, 1, 4), name="scores_body",
    )
    packs = along_ctx(pack)
    v_before, v_after = lax.ppermute(vlast, "ctx", up), lax.ppermute(vfirst, "ctx", down)
    (conv,) = call(simple(conv_body), [((T, E), BF)], row_fwd, seg_col, v, v_before, v_after, far_in=(0, 1), far_out=(0,))
    kt, mixer, p_all, w_all, pi_all = call(
        simple(newton_body), [((L, E), F32), ((L, E), F32)] + [((NEWTON, L, E), F32)] * 3, land, far_out=range(5), us=5.5, mem=10
    )
    n_pieces = D // R if aligned else 1
    res = call(
        functools.partial(mid_body, nc, n_pieces, row_bits, nc),
        [((T, E), BF), ((L, E), F32), ((L, E), F32), ((L, META), F32), ((T, E), BF), ((T, D), BF), ((T, E), BF)]
        + [((REACH, E), BF)] * 2
        + [((L, E), BF), ((T, D), F32), ((T, D), BF), ((8, D), F32), ((1, 2 * FL), F32)]
        + [((2, D // 2, FL), BF)] * 4,
        where, *packs, mixer, ktok, conv, land_far, x, cot, perm, vec, fb, qkv, w_full, ud,
        us=24.0,
        mem=30,
        smem=(0,),
        far_in=range(1, nc + 10),
        raw_in=(nc + 10, nc + 11, nc + 12),
        far_out=(5,),
        scratch=[
            pltpu.VMEM((2, D, C), BF),
            pltpu.VMEM((2, D, FL), BF),
            pltpu.VMEM((2, D, FL), BF),
            pltpu.VMEM((T, 2 * FL), BF),
            pltpu.VMEM((T, 2 * FL), F32),
            pltpu.VMEM((L, E), F32),
            pltpu.VMEM((1, T, E), BF),
            pltpu.SemaphoreType.DMA((2, 2 * n_pieces)),
            pltpu.SemaphoreType.DMA((2,)),
        ],
        name="mid_body",
    )
    gq, lk_part, lval, land_scale, mixed, y, gm, gfirst, glast, gmix0, grad_first, grad_branch, sums, fb_grad = res[:14]
    keep_up, send_up, keep_down, send_down = res[14:]

    every = slice(None)

    def cores_sum(keep, send):
        got = swap(send, *core_bit)
        for bit in reversed(chip_bits[1:]):
            half = keep.shape[1] // 2
            more = swap(add(keep[:, half:], got[:, half:]), *bit)
            keep, got = add(keep[:, :half], got[:, :half]), more
        return keep, got

    bit = chip_bits[0]
    low_rows, high_rows = slice(0, nc * R), slice(nc * R, 2 * nc * R)

    def one_start(keep, got):
        (other,) = combine([[[(0, (1,)), (1, (1,))]]], keep, got, near=aligned)
        return other, swap(other, "tp", 1)

    def two_start(keep, got):
        (send,) = combine([[[(0, (every, high_rows)), (1, (every, high_rows))]]], keep, got, near=aligned)
        return send, swap(send, *bit)

    def one_next(keep, got, more):
        (send,) = combine([[[(0, (0, high_rows)), (1, (0, high_rows)), (2, (high_rows,))]]], keep, got, more, near=aligned)
        return send, swap(send, *bit)

    def two_next(keep, got, more):
        (send,) = combine([[[(0, (1, low_rows)), (1, (1, low_rows)), (2, (1,))]]], keep, got, more, near=aligned)
        return send, swap(send, "tp", 1)

    def ctx_cuts(one, two):
        plan = []
        for p in range(nc):
            rows = slice(p * R, (p + 1) * R)
            plan.append(
                [
                    [(0, (0, rows)), (1, (0, rows)), (2, (rows,)), (3, (rows,))],
                    [(4, (0, rows)), (5, (0, rows)), (6, (0, rows)), (7, (rows,))],
                ]
            )
        return combine(plan, *one, *two, near=aligned)

    def ctx_swap(cuts):
        return [cuts[0]] + [swap(cuts[p], "ctx", p) for p in range(1, nc)]

    def pairs(values):
        while len(values) > 1:
            values = [a + b for a, b in zip(values[::2], values[1::2])]
        return values[0]

    def total(parts):
        return sum(p.astype(F32) for p in parts)

    gmixes = along_ctx(gmix0)
    down2 = cores_sum(keep_down, send_down)
    up2 = cores_sum(keep_up, send_up)
    down2, up2 = later((down2, up2), *gmixes)
    g_before, g_after = lax.ppermute(glast, "ctx", up), lax.ppermute(gfirst, "ctx", down)
    down_sent, down_more = two_start(*down2)
    up_sent, up_more = one_start(*up2)
    res = call(
        functools.partial(key_back_body, nc),
        [((L, E), F32), ((T, E), BF), ((T, E), BF), ((LL, 2 * E), F32)] + [((LL, 2 * E), BF)] * (nc - 1),
        where, *later(gmixes, up_sent, down_sent), mixer, lval, ekey, land_scale, qkv, land_far, lk_part,
        smem=(0,),
        far_in=(nc + 1, nc + 3, nc + 5, nc + 6),
        scratch=[pltpu.VMEM((L, 2 * E), F32)],
        us=3.0,
        mem=12,
        name="key_back_body",
    )
    gmix, gv, gk, own_part = res[:4]
    parts = [own_part] + [swap(a, "ctx", p + 1) for p, a in enumerate(res[4:])]
    own_mix, gvc, tap_all = call(
        functools.partial(back_body, 9), [((LL, 2 * E), F32), ((T, E), BF), ((H, T + 2 * META), F32)],
        land_far, kt, p_all, w_all, pi_all, mixer, gmix, lval, where,
        row_back, seg_col, gm, g_before, g_after, qkv, v_before, v_after,
        smem=(8,),
        far_in=(0, 1, 2, 3, 4, 5, 9, 10, 14, 15, 16),
        scratch=[pltpu.VMEM((L, 2 * E), F32)],
        us=11.0,
        mem=18,
        name="back_body",
    )
    gq, gk, gv, hb_grad, keep1, send1, keep2, send2 = call(
        functools.partial(grad_body, nc),
        [((T, E), BF)] * 3 + [((2, E), F32)] + [((2, D // 2, 2 * C), BF)] * 4,
        *parts, own_mix, gq, gk, gv, gvc, x, grad_branch, mixed,
        far_in=(nc + 5,),
        us=3.0,
        mem=10,
        name="grad_body",
    )
    down_sent2, down_more2 = two_next(*down2, later(down_more, hb_grad))
    up_sent2, up_more2 = one_next(*up2, later(up_more, hb_grad))
    vo2 = cores_sum(keep2, send2)
    qk2 = cores_sum(keep1, send1)
    vo_sent, vo_more = two_start(*later(vo2, down_sent2, up_sent2))
    qk_sent, qk_more = one_start(*later(qk2, down_sent2, up_sent2))
    rows = -(-KW // 8) * 8 + (7 * D + FL) // META
    rows += -rows % 8
    (small,) = call(
        functools.partial(small_body, rows), [((2, rows, META), F32)], later(tap_all, vo_sent, qk_sent), hb_grad, fb_grad, sums, perm,
        far_in=(0, 4), mem=12, name="small_body",
    )
    small_ctx = along_ctx(small)
    (gx,) = call(
        simple(input_grad_body), [((T, D), BF)], later(gq, small), gk, gv, grad_first, perm, w_full,
        far_in=(4, 5), far_out=(0,), us=4.0, mem=14,
    )
    cuts_ud = ctx_cuts((*up2, *later((up_more, up_more2), gx)), (*down2, down_more, down_more2))
    ctx_ud = ctx_swap(cuts_ud)
    small = pairs(later(small_ctx, *cuts_ud))
    small_got = swap(small, *core_bit)
    vo_sent2, vo_more2 = two_next(*vo2, later(vo_more, small))
    qk_sent2, qk_more2 = one_next(*qk2, later(qk_more, small))
    small = small + later(small_got, vo_sent2, qk_sent2)
    for extra in chip_bits[1:]:
        small = small + swap(small, *extra)
    small_got = [swap(small[0], *bit), swap(small[1], "tp", 1), swap_both(small[1], bit[1])]
    y = later(y, vo_sent2, qk_sent2)
    cuts_q = ctx_cuts((*qk2, qk_more, qk_more2), (*vo2, vo_more, vo_more2))
    ctx_q = ctx_swap(cuts_q)
    small_got = later(small_got, *cuts_q)
    ud_grad = total(later(ctx_ud, *cuts_q))
    qo = total(ctx_q)
    conv_grad, hb_out, fb_out, gains_out, offsets_out = call(
        simple(small_out_body),
        [((KW, HL), F32), ((2, C), F32), ((1, FL), F32), ((2, D), F32), ((4, D), F32)],
        small, *small_got,
    )

    def place(mine):
        other = swap(mine, "tp", 1)
        first = t_i == 0
        return jnp.stack([jnp.where(first, mine, other), jnp.where(first, other, mine)])

    return (
        place(y),
        place(gx),
        qo[:, : 3 * C].reshape(R, 3, C),
        qo[:, 3 * C :],
        ud_grad[:, :FL],
        ud_grad[:, FL:],
        conv_grad,
        hb_out,
        fb_out[0],
        gains_out,
        offsets_out,
    )


def solution(mesh):
    placed = (
        P("fsdp", "ctx", None),
        P("fsdp", "ctx", None),
        P("fsdp", "ctx"),
        P("fsdp", "ctx"),
        P(("fsdp", "ctx"), None, "tp"),
        P(("fsdp", "ctx"), "tp"),
        P(("fsdp", "ctx"), "tp"),
        P(("fsdp", "ctx"), "tp"),
        P(None, "tp"),
        P(None, "tp"),
        P("tp"),
        P(),
        P(),
    )
    return jax.shard_map(
        local,
        mesh=mesh,
        in_specs=placed,
        out_specs=placed[:2] + placed[4:],
        check_vma=False,
    )
```

time: 400 us -> 281 us (0.70)
  the two profiles are of different devices: /device:TPU:0 before, /device:TPU:20 now
where the time goes in v2:
time: 281 us; the launch traced here: 276 us
  waiting for transfers between devices  85.9 us (31%)
  Pallas kernels  78.4 us (28%)
  starting transfers between devices  72.4 us (26%)
  between operations  15.3 us (5%)
  other arithmetic  10.8 us (4%)
  local copies, waits for them, and re-layouts  9.96 us (4%)
  matrix products  3.55 us (1%)
    pallas_call x21, Pallas kernels, call(): pl.pallas_call(inner, out_shape=[r(*o) for r, o in zip(res, outs)], in_sp...  78.4 us
    ppermute x48, waiting for transfers between devices, swap(): lax.ppermute(a, axis, [(i, i ^ mask) for i in range(lax.axis_size(axis))])  64.2 us
    ppermute x48, starting transfers between devices, swap(): lax.ppermute(a, axis, [(i, i ^ mask) for i in range(lax.axis_size(axis))])  56.4 us
    ppermute x2, waiting for transfers between devices, swap_both(): lax.ppermute(a, ('fsdp', 'tp'), [(2 * i + j, 2 * (i ^ mask) + (j ^ 1)) fo...  12.4 us
    all_gather x1, waiting for transfers between devices, local(): lax.all_gather(jnp.concatenate([w_up, w_down], axis=1), ('fsdp', 'ctx', '...  9.28 us
  transfers between devices with their start and end apart: 55, of which 19 were waited for; matrix products, arithmetic and copies ran while one was open for 7% of the time, Pallas kernels for 20%

profile of v2, /device:TPU:20, one launch (start us, length us, event | category | flops | bytes accessed | tf_op | source)
XLA Modules:
  0.0 276.3 jit_solution(11079164227460425540)
XLA Ops:
  10.6 3.5 %collective-permute-start.2 = (bf16[48,1536]{1,0:T(8,128)(2,1)S(1)}, bf16[48,1536]{1,0:T(8,128)(2,1)S(1)}, u32[]{:S(2)}, u32[]{:S(2)}) collective-permute-start(bf16[48,1536]{1,0:T(8,128)(2,1)S(1)} %constant_dynamic-update-slice_fusion), channel_id=1, source_target_pairs={{0,4},{2,6},{4,0},{6,2},{1,5},{3,7},{5,1},{7,3},{8,12},{10,14},{12... | collective-permute-start | bytes 442376 | tf_op jit(solution)/shard_map/ppermute | solution.py:33
  18.6 4.7 %collective-permute-done.3 = bf16[48,1536]{1,0:T(8,128)(2,1)S(1)} collective-permute-done((bf16[48,1536]{1,0:T(8,128)(2,1)S(1)}, bf16[48,1536]{1,0:T(8,128)(2,1)S(1)}, u32[]{:S(2)}, u32[]{:S(2)}) %collective-permute-start.3) | collective-permute-done | bytes 147488 | tf_op jit(solution)/shard_map/ppermute | solution.py:33
  30.2 12.4 %collective-permute-done.8.refs_10_ = bf16[192,1536]{1,0:T(8,128)(2,1)S(1)} collective-permute-done((bf16[192,1536]{1,0:T(8,128)(2,1)S(1)}, bf16[192,1536]{1,0:T(8,128)(2,1)S(1)}, u32[]{:S(2)}, u32[]{:S(2)}) %collective-permute-start.8) | collective-permute-done | bytes 589856 | tf_op jit(solution)/shard_map/ppermute | solution.py:38
  42.7 12.7 %collective-permute-done.7.refs_9_ = bf16[192,1536]{1,0:T(8,128)(2,1)S(1)} collective-permute-done((bf16[192,1536]{1,0:T(8,128)(2,1)S(1)}, bf16[192,1536]{1,0:T(8,128)(2,1)S(1)}, u32[]{:S(2)}, u32[]{:S(2)}) %collective-permute-start.7) | collective-permute-done | bytes 589856 | tf_op jit(solution)/shard_map/ppermute | solution.py:33
  59.5 5.0 %proj_body.1 = (bf16[256,768]{1,0:T(8,128)(2,1)S(1)}, bf16[256,768]{1,0:T(8,128)(2,1)S(1)}, bf16[256,768]{1,0:T(8,128)(2,1)S(1)}, bf16[3,256,768]{2,1,0:T(8,128)...) custom-call(bf16[256,768]{1,0:T(8,128)(2,1)S(1)} %fusion.4.refs_0_.r, ...), custom_call_target="tpu_custom_call" | custom-call | flops 20000000 | bytes 1024 | tf_op jit(solution)/shard_map/proj_body/pallas_call | solution.py:177
  64.4 2.8 %collective-permute-start.13 = (bf16[16,1664]{1,0:T(8,128)(2,1)S(1)}, bf16[16,1664]{1,0:T(8,128)(2,1)S(1)}, u32[]{:S(2)}, u32[]{:S(2)}) collective-permute-start(bf16[16,1664]{1,0:T(8,128)(2,1)S(1)} %get-tuple-element.144.refs_5_), channel_id=1, source_target_pairs={{0,6},{2,4},{4,2},{6,0},{1,7},{3,5},{5,3},{7,1},{8,14},{10,12},{12... | collective-permute-start | bytes 159752 | tf_op jit(solution)/shard_map/ppermute | solution.py:33
  67.3 6.2 %collective-permute-start.12 = (bf16[16,1664]{1,0:T(8,128)(2,1)S(1)}, bf16[16,1664]{1,0:T(8,128)(2,1)S(1)}, u32[]{:S(2)}, u32[]{:S(2)}) collective-permute-start(bf16[16,1664]{1,0:T(8,128)(2,1)S(1)} %get-tuple-element.144.refs_5_), channel_id=1, source_target_pairs={{0,4},{2,6},{4,0},{6,2},{1,5},{3,7},{5,1},{7,3},{8,12},{10,14},{12... | collective-permute-start | bytes 159752 | tf_op jit(solution)/shard_map/ppermute | solution.py:33
  73.7 3.9 %collective-permute-start.17 = (bf16[16,896]{1,0:T(8,128)(2,1)S(1)}, bf16[16,896]{1,0:T(8,128)(2,1)S(1)}, u32[]{:S(2)}, u32[]{:S(2)}) collective-permute-start(bf16[16,896]{1,0:T(8,128)(2,1)S(1)} %get-tuple-element.149), channel_id=1, source_target_pairs={{0,2},{2,4},{4,6},{1,3},{3,5},{5,7},{8,10},{10,12},{12,14},{9,11},... | collective-permute-start | bytes 86024 | tf_op jit(solution)/shard_map/ppermute | solution.py:912
  83.2 3.8 %collective-permute-start.15 = (bf16[64,896]{1,0:T(8,128)(2,1)S(1)}, bf16[64,896]{1,0:T(8,128)(2,1)S(1)}, u32[]{:S(2)}, u32[]{:S(2)}) collective-permute-start(bf16[64,896]{1,0:T(8,128)(2,1)S(1)} %get-tuple-element.145.refs_1_), channel_id=1, source_target_pairs={{0,4},{2,6},{4,0},{6,2},{1,5},{3,7},{5,1},{7,3},{8,12},{10,14},{12... | collective-permute-start | bytes 344072 | tf_op jit(solution)/shard_map/ppermute | solution.py:33
  90.9 7.4 %newton_body.1 = (f32[64,768]{1,0:T(8,128)}, f32[64,768]{1,0:T(8,128)}, f32[6,64,768]{2,1,0:T(8,128)}, f32[6,64,768]{2,1,0:T(8,128)}, f32[6,64,768]{2,1,0:T(8,128)}) custom-call(bf16[64,1664]{1,0:T(8,128)(2,1)S(1)} %get-tuple-element.146.refs_0_), custom_call_target="tpu_custom_call" | custom-call | flops 55000000 | bytes 1024 | tf_op jit(solution)/shard_map/newton_body/pallas_call | solution.py:177
  99.2 4.8 %collective-permute-done.15.refs_3_ = bf16[64,896]{1,0:T(8,128)(2,1)S(1)} collective-permute-done((bf16[64,896]{1,0:T(8,128)(2,1)S(1)}, bf16[64,896]{1,0:T(8,128)(2,1)S(1)}, u32[]{:S(2)}, u32[]{:S(2)}) %collective-permute-start.15) | collective-permute-done | bytes 114720 | tf_op jit(solution)/shard_map/ppermute | solution.py:33
  104.0 9.3 %all-gather.2.cloned.1.call-done = bf16[1536,3072]{1,0:T(8,128)(2,1)} async-done(((bf16[48,3072]{1,0:T(8,128)(2,1)}), bf16[1536,3072]{1,0:T(8,128)(2,1)}) %all-gather.2.cloned.1.call-update) | async-done | bytes 9437200 | tf_op jit(solution)/shard_map/all_gather | solution.py:835
  113.3 21.6 %mid_body.1 = (bf16[256,768]{1,0:T(8,128)(2,1)S(1)}, f32[64,768]{1,0:T(8,128)S(1)}, f32[64,768]{1,0:T(8,128)S(1)}, f32[64,128]{1,0:T(8,128)S(1)}, bf16[256,768]{...) custom-call(s32[3]{0:T(128)S(1)} %pad_add_fusion.refs_0_.refs_8_, ...), custom_call_target="tpu_custom_call" | custom-call | flops 240000000 | bytes 1024 | tf_op jit(solution)/shard_map/mid_body/pallas_call | solution.py:177
  136.1 4.9 %collective-permute-start.20 = (bf16[64,768]{1,0:T(8,128)(2,1)S(1)}, bf16[64,768]{1,0:T(8,128)(2,1)S(1)}, u32[]{:S(2)}, u32[]{:S(2)}) collective-permute-start(bf16[64,768]{1,0:T(8,128)(2,1)S(1)} %get-tuple-element.164.refs_1_), channel_id=1, source_target_pairs={{0,4},{2,6},{4,0},{6,2},{1,5},{3,7},{5,1},{7,3},{8,12},{10,14},{12... | collective-permute-start | bytes 294920 | tf_op jit(solution)/shard_map/ppermute | solution.py:33
  141.1 5.7 %collective-permute-done.20.refs_3_ = bf16[64,768]{1,0:T(8,128)(2,1)S(1)} collective-permute-done((bf16[64,768]{1,0:T(8,128)(2,1)S(1)}, bf16[64,768]{1,0:T(8,128)(2,1)S(1)}, u32[]{:S(2)}, u32[]{:S(2)}) %collective-permute-start.20) | collective-permute-done | bytes 98336 | tf_op jit(solution)/shard_map/ppermute | solution.py:33
  150.8 4.5 %collective-permute-start.27 = (bf16[16,768]{1,0:T(8,128)(2,1)S(1)}, bf16[16,768]{1,0:T(8,128)(2,1)S(1)}, u32[]{:S(2)}, u32[]{:S(2)}) collective-permute-start(bf16[16,768]{1,0:T(8,128)(2,1)S(1)} %get-tuple-element.182), channel_id=1, source_target_pairs={{0,2},{2,4},{4,6},{1,3},{3,5},{5,7},{8,10},{10,12},{12,14},{9,11},... | collective-permute-start | bytes 73736 | tf_op jit(solution)/shard_map/ppermute | solution.py:1003
  157.4 4.4 %key_back_body.1 = (f32[64,768]{1,0:T(8,128)S(1)}, bf16[256,768]{1,0:T(8,128)(2,1)S(1)}, bf16[256,768]{1,0:T(8,128)(2,1)S(1)}, f32[16,1536]{1,0:T(8,128)S(1)}, b...) custom-call(s32[3]{0:T(128)S(1)} %pad_add_fusion.refs_0_.refs_8_, ...), custom_call_target="tpu_custom_call" | custom-call | flops 30000000 | bytes 1024 | tf_op jit(solution)/shard_map/key_back_body/pallas_call | solution.py:177
  165.5 17.8 %back_body.1 = (f32[16,1536]{1,0:T(8,128)S(1)}, bf16[256,768]{1,0:T(8,128)(2,1)S(1)}, f32[12,512]{1,0:T(8,128)S(1)}) custom-call(bf16[64,1664]{1,0:T(8,128)(2,1)} %get-tuple-element.151.refs_8_.refs_10_.refs_0_, f32[64,768]{1,0:T(8,128)} %get-tuple-element.176.refs_1_, f32[6,64,768]{2,1,0:T(8,128)} %get-tuple-element.177.refs_2_, ...), custom_call_target="tpu_custom_call" | custom-call | flops 110000000 | bytes 1024 | tf_op jit(solution)/shard_map/back_body/pallas_call | solution.py:177
  183.3 2.9 %grad_body.1 = (bf16[256,768]{1,0:T(8,128)(2,1)S(1)}, bf16[256,768]{1,0:T(8,128)(2,1)S(1)}, bf16[256,768]{1,0:T(8,128)(2,1)S(1)}, f32[2,768]{1,0:T(2,128)S(1)}, ...) custom-call(f32[16,1536]{1,0:T(8,128)S(1)} %get-tuple-element.172.re, ...), custom_call_target="tpu_custom_call" | custom-call | flops 30000000 | bytes 1024 | tf_op jit(solution)/shard_map/grad_body/pallas_call | solution.py:177
  195.5 7.7 %collective-permute-done.37.refs_3_ = bf16[192,1536]{1,0:T(8,128)(2,1)S(1)} collective-permute-done((bf16[192,1536]{1,0:T(8,128)(2,1)S(1)}, bf16[192,1536]{1,0:T(8,128)(2,1)S(1)}, u32[]{:S(2)}, u32[]{:S(2)}) %collective-permute-start.37) | collective-permute-done | bytes 589856 | tf_op jit(solution)/shard_map/ppermute | solution.py:33
  207.0 5.7 %input_grad_body.1 = bf16[256,768]{1,0:T(8,128)(2,1)} custom-call(bf16[256,768]{1,0:T(8,128)(2,1)S(1)} %get-tuple-element.207.refs_0_, bf16[256,768]{1,0:T(8,128)(2,1)S(1)} %get-tuple-element.208.refs_1_, bf16[256,768]{1,0:T(8,128)(2,1)S(1)} %get-tuple-element.209.refs_2_, f32[256,768]{1,0:T(8,128)S(1)} %get-tuple-element.210.refs_3_, ...), custom_call_target="tpu_custom_call" | custom-call | flops 40000000 | bytes 1024 | tf_op jit(solution)/shard_map/input_grad_body/pallas_call | solution.py:177
  222.5 2.8 %collective-permute-start.47 = (bf16[48,3072]{1,0:T(8,128)(2,1)}, bf16[48,3072]{1,0:T(8,128)(2,1)}, u32[]{:S(2)}, u32[]{:S(2)}) collective-permute-start(bf16[48,3072]{1,0:T(8,128)(2,1)} %copy-done.21), channel_id=1, source_target_pairs={{0,2},{2,0},{4,6},{6,4},{1,3},{3,1},{5,7},{7,5},{8,10},{10,8},{12,... | collective-permute-start | bytes 884744 | tf_op jit(solution)/shard_map/ppermute | solution.py:33
  242.5 8.9 %collective-permute-done.48 = bf16[48,3072]{1,0:T(8,128)(2,1)} collective-permute-done((bf16[48,3072]{1,0:T(8,128)(2,1)}, bf16[48,3072]{1,0:T(8,128)(2,1)}, u32[]{:S(2)}, u32[]{:S(2)}) %collective-permute-start.48) | collective-permute-done | bytes 294944 | tf_op jit(solution)/shard_map/ppermute | solution.py:33
  252.5 8.4 %collective-permute-done.49 = bf16[48,3072]{1,0:T(8,128)(2,1)} collective-permute-done((bf16[48,3072]{1,0:T(8,128)(2,1)}, bf16[48,3072]{1,0:T(8,128)(2,1)}, u32[]{:S(2)}, u32[]{:S(2)}) %collective-permute-start.49) | collective-permute-done | bytes 294944 | tf_op jit(solution)/shard_map/ppermute | solution.py:33
  (247 shorter events, 89.1 us)
Async XLA Ops:
  7.3 106.0 %all-gather.2.cloned.1.call-start = ((), (), s32[]{:S(2)}) async-start(), calls=%async_computation | async-start | bytes 9732096 | tf_op jit(solution)/shard_map/all_gather | solution.py:835
  25.4 17.2 %collective-permute-start.8 = (bf16[192,1536]{1,0:T(8,128)(2,1)S(1)}, bf16[192,1536]{1,0:T(8,128)(2,1)S(1)}, u32[]{:S(2)}, u32[]{:S(2)}) collective-permute-start(bf16[192,1536]{1,0:T(8,128)(2,1)S(1)} %pad_maximum_fusion.2.refs_5_), channel_id=1, source_target_pairs={{0,17},{1,16},{8,25},{9,24},{16,1},{17,0},{24,9},{25,8},{2,19},{3,... | collective-permute-start | bytes 1769480 | tf_op jit(solution)/shard_map/ppermute | solution.py:38
  26.9 28.4 %collective-permute-start.7 = (bf16[192,1536]{1,0:T(8,128)(2,1)S(1)}, bf16[192,1536]{1,0:T(8,128)(2,1)S(1)}, u32[]{:S(2)}, u32[]{:S(2)}) collective-permute-start(bf16[192,1536]{1,0:T(8,128)(2,1)S(1)} %pad_maximum_fusion.2.refs_5_), channel_id=1, source_target_pairs={{0,1},{1,0},{2,3},{3,2},{4,5},{5,4},{6,7},{7,6},{8,9},{9,8},{10,11... | collective-permute-start | bytes 1769480 | tf_op jit(solution)/shard_map/ppermute | solution.py:33
  28.6 28.7 %collective-permute-start.4 = (bf16[192,1536]{1,0:T(8,128)(2,1)S(1)}, bf16[192,1536]{1,0:T(8,128)(2,1)S(1)}, u32[]{:S(2)}, u32[]{:S(2)}) collective-permute-start(bf16[192,1536]{1,0:T(8,128)(2,1)S(1)} %pad_maximum_fusion.2.refs_5_), channel_id=1, source_target_pairs={{0,16},{8,24},{16,0},{24,8},{1,17},{9,25},{17,1},{25,9},{2,18},{10... | collective-permute-start | bytes 1769480 | tf_op jit(solution)/shard_map/ppermute | solution.py:33
  30.2 28.1 %collective-permute-start.5 = (bf16[192,1536]{1,0:T(8,128)(2,1)S(1)}, bf16[192,1536]{1,0:T(8,128)(2,1)}, u32[]{:S(2)}, u32[]{:S(2)}) collective-permute-start(bf16[192,1536]{1,0:T(8,128)(2,1)S(1)} %pad_maximum_fusion.2.refs_5_), channel_id=1, source_target_pairs={{0,8},{8,0},{16,24},{24,16},{1,9},{9,1},{17,25},{25,17},{2,10},{10... | collective-permute-start | bytes 1769480 | tf_op jit(solution)/shard_map/ppermute | solution.py:33
  82.6 16.6 %collective-permute-start.16 = (bf16[64,896]{1,0:T(8,128)(2,1)S(1)}, bf16[64,896]{1,0:T(8,128)(2,1)S(1)}, u32[]{:S(2)}, u32[]{:S(2)}) collective-permute-start(bf16[64,896]{1,0:T(8,128)(2,1)S(1)} %get-tuple-element.145.refs_1_), channel_id=1, source_target_pairs={{0,6},{2,4},{4,2},{6,0},{1,7},{3,5},{5,3},{7,1},{8,14},{10,12},{12... | collective-permute-start | bytes 344072 | tf_op jit(solution)/shard_map/ppermute | solution.py:33
  83.2 20.8 %collective-permute-start.15 = (bf16[64,896]{1,0:T(8,128)(2,1)S(1)}, bf16[64,896]{1,0:T(8,128)(2,1)S(1)}, u32[]{:S(2)}, u32[]{:S(2)}) collective-permute-start(bf16[64,896]{1,0:T(8,128)(2,1)S(1)} %get-tuple-element.145.refs_1_), channel_id=1, source_target_pairs={{0,4},{2,6},{4,0},{6,2},{1,5},{3,7},{5,1},{7,3},{8,12},{10,14},{12... | collective-permute-start | bytes 344072 | tf_op jit(solution)/shard_map/ppermute | solution.py:33
  87.0 17.0 %collective-permute-start.14 = (bf16[64,896]{1,0:T(8,128)(2,1)S(1)}, bf16[64,896]{1,0:T(8,128)(2,1)S(1)}, u32[]{:S(2)}, u32[]{:S(2)}) collective-permute-start(bf16[64,896]{1,0:T(8,128)(2,1)S(1)} %get-tuple-element.145.refs_1_), channel_id=1, source_target_pairs={{0,2},{2,0},{4,6},{6,4},{1,3},{3,1},{5,7},{7,5},{8,10},{10,8},{12,... | collective-permute-start | bytes 344072 | tf_op jit(solution)/shard_map/ppermute | solution.py:33
  147.8 39.0 %collective-permute-start.31 = (bf16[384,1536]{1,0:T(8,128)(2,1)S(1)}, bf16[384,1536]{1,0:T(8,128)(2,1)S(1)}, u32[]{:S(2)}, u32[]{:S(2)}) collective-permute-start(bf16[384,1536]{1,0:T(8,128)(2,1)S(1)} %sum_body.10), channel_id=1, source_target_pairs={{0,1},{1,0},{2,3},{3,2},{4,5},{5,4},{6,7},{7,6},{8,9},{9,8},{10,11... | collective-permute-start | bytes 3538952 | tf_op jit(solution)/shard_map/ppermute | solution.py:33
  149.3 37.5 %collective-permute-start.30 = (bf16[2,192,1536]{2,1,0:T(8,128)(2,1)S(1)}, bf16[2,192,1536]{2,1,0:T(8,128)(2,1)S(1)}, u32[]{:S(2)}, u32[]{:S(2)}) collective-permute-start(bf16[2,192,1536]{2,1,0:T(8,128)(2,1)S(1)} %sum_body.11), channel_id=1, source_target_pairs={{0,16},{8,24},{16,0},{24,8},{1,17},{9,25},{17,1},{25,9},{2,18},{10... | collective-permute-start | bytes 3538952 | tf_op jit(solution)/shard_map/ppermute | solution.py:33
  161.8 21.4 %collective-permute-start.24 = (bf16[16,1536]{1,0:T(8,128)(2,1)S(1)}, bf16[16,1536]{1,0:T(8,128)(2,1)S(1)}, u32[]{:S(2)}, u32[]{:S(2)}) collective-permute-start(bf16[16,1536]{1,0:T(8,128)(2,1)S(1)} %get-tuple-element.173), channel_id=1, source_target_pairs={{0,2},{2,0},{4,6},{6,4},{1,3},{3,1},{5,7},{7,5},{8,10},{10,8},{12,... | collective-permute-start | bytes 147464 | tf_op jit(solution)/shard_map/ppermute | solution.py:33
  163.9 19.3 %collective-permute-start.25 = (bf16[16,1536]{1,0:T(8,128)(2,1)S(1)}, bf16[16,1536]{1,0:T(8,128)(2,1)S(1)}, u32[]{:S(2)}, u32[]{:S(2)}) collective-permute-start(bf16[16,1536]{1,0:T(8,128)(2,1)S(1)} %get-tuple-element.174), channel_id=1, source_target_pairs={{0,4},{2,6},{4,0},{6,2},{1,5},{3,7},{5,1},{7,3},{8,12},{10,14},{12... | collective-permute-start | bytes 147464 | tf_op jit(solution)/shard_map/ppermute | solution.py:33
  164.6 18.7 %collective-permute-start.26 = (bf16[16,1536]{1,0:T(8,128)(2,1)S(1)}, bf16[16,1536]{1,0:T(8,128)(2,1)S(1)}, u32[]{:S(2)}, u32[]{:S(2)}) collective-permute-start(bf16[16,1536]{1,0:T(8,128)(2,1)S(1)} %get-tuple-element.175), channel_id=1, source_target_pairs={{0,6},{2,4},{4,2},{6,0},{1,7},{3,5},{5,3},{7,1},{8,14},{10,12},{12... | collective-permute-start | bytes 147464 | tf_op jit(solution)/shard_map/ppermute | solution.py:33
  187.0 16.2 %collective-permute-start.37 = (bf16[192,1536]{1,0:T(8,128)(2,1)S(1)}, bf16[192,1536]{1,0:T(8,128)(2,1)S(1)}, u32[]{:S(2)}, u32[]{:S(2)}) collective-permute-start(bf16[192,1536]{1,0:T(8,128)(2,1)S(1)} %sum_body.13), channel_id=1, source_target_pairs={{0,16},{8,24},{16,0},{24,8},{1,17},{9,25},{17,1},{25,9},{2,18},{10... | collective-permute-start | bytes 1769480 | tf_op jit(solution)/shard_map/ppermute | solution.py:33
  187.9 17.0 %collective-permute-start.38 = (bf16[192,1536]{1,0:T(8,128)(2,1)S(1)}, bf16[192,1536]{1,0:T(8,128)(2,1)S(1)}, u32[]{:S(2)}, u32[]{:S(2)}) collective-permute-start(bf16[192,1536]{1,0:T(8,128)(2,1)S(1)} %sum_body.12), channel_id=1, source_target_pairs={{0,1},{1,0},{2,3},{3,2},{4,5},{5,4},{6,7},{7,6},{8,9},{9,8},{10,11... | collective-permute-start | bytes 1769480 | tf_op jit(solution)/shard_map/ppermute | solution.py:33
  189.3 25.8 %collective-permute-start.32 = (bf16[2,192,768]{2,1,0:T(8,128)(2,1)S(1)}, bf16[2,192,768]{2,1,0:T(8,128)(2,1)S(1)}, u32[]{:S(2)}, u32[]{:S(2)}) collective-permute-start(bf16[2,192,768]{2,1,0:T(8,128)(2,1)S(1)} %sum_body.14), channel_id=1, source_target_pairs={{0,16},{8,24},{16,0},{24,8},{1,17},{9,25},{17,1},{25,9},{2,18},{10... | collective-permute-start | bytes 1769480 | tf_op jit(solution)/shard_map/ppermute | solution.py:33
  191.0 25.9 %collective-permute-start.39 = (bf16[384,768]{1,0:T(8,128)(2,1)S(1)}, bf16[384,768]{1,0:T(8,128)(2,1)S(1)}, u32[]{:S(2)}, u32[]{:S(2)}) collective-permute-start(bf16[384,768]{1,0:T(8,128)(2,1)S(1)} %sum_body.15), channel_id=1, source_target_pairs={{0,1},{1,0},{2,3},{3,2},{4,5},{5,4},{6,7},{7,6},{8,9},{9,8},{10,11... | collective-permute-start | bytes 1769480 | tf_op jit(solution)/shard_map/ppermute | solution.py:33
  194.3 19.1 %collective-permute-start.36 = (f32[2,96,128]{2,1,0:T(8,128)S(1)}, f32[2,96,128]{2,1,0:T(8,128)S(1)}, u32[]{:S(2)}, u32[]{:S(2)}) collective-permute-start(f32[2,96,128]{2,1,0:T(8,128)S(1)} %small_body.1), channel_id=1, source_target_pairs={{0,6},{2,4},{4,2},{6,0},{1,7},{3,5},{5,3},{7,1},{8,14},{10,12},{12... | collective-permute-start | bytes 294920 | tf_op jit(solution)/shard_map/ppermute | solution.py:33
  222.5 20.0 %collective-permute-start.47 = (bf16[48,3072]{1,0:T(8,128)(2,1)}, bf16[48,3072]{1,0:T(8,128)(2,1)}, u32[]{:S(2)}, u32[]{:S(2)}) collective-permute-start(bf16[48,3072]{1,0:T(8,128)(2,1)} %copy-done.21), channel_id=1, source_target_pairs={{0,2},{2,0},{4,6},{6,4},{1,3},{3,1},{5,7},{7,5},{8,10},{10,8},{12,... | collective-permute-start | bytes 884744 | tf_op jit(solution)/shard_map/ppermute | solution.py:33
  225.9 25.5 %collective-permute-start.48 = (bf16[48,3072]{1,0:T(8,128)(2,1)}, bf16[48,3072]{1,0:T(8,128)(2,1)}, u32[]{:S(2)}, u32[]{:S(2)}) collective-permute-start(bf16[48,3072]{1,0:T(8,128)(2,1)} %copy-done.20), channel_id=1, source_target_pairs={{0,4},{2,6},{4,0},{6,2},{1,5},{3,7},{5,1},{7,3},{8,12},{10,14},{12... | collective-permute-start | bytes 884744 | tf_op jit(solution)/shard_map/ppermute | solution.py:33
  227.9 33.0 %collective-permute-start.49 = (bf16[48,3072]{1,0:T(8,128)(2,1)}, bf16[48,3072]{1,0:T(8,128)(2,1)}, u32[]{:S(2)}, u32[]{:S(2)}) collective-permute-start(bf16[48,3072]{1,0:T(8,128)(2,1)} %copy-done.19), channel_id=1, source_target_pairs={{0,6},{2,4},{4,2},{6,0},{1,7},{3,5},{5,3},{7,1},{8,14},{10,12},{12... | collective-permute-start | bytes 884744 | tf_op jit(solution)/shard_map/ppermute | solution.py:33
  238.1 27.4 %collective-permute-start.40 = (bf16[256,768]{1,0:T(8,128)(2,1)}, bf16[256,768]{1,0:T(8,128)(2,1)S(1)}, u32[]{:S(2)}, u32[]{:S(2)}) collective-permute-start(bf16[256,768]{1,0:T(8,128)(2,1)} %get-tuple-element.223), channel_id=1, source_target_pairs={{0,1},{1,0},{2,3},{3,2},{4,5},{5,4},{6,7},{7,6},{8,9},{9,8},{10,11... | collective-permute-start | bytes 1179656 | tf_op jit(solution)/shard_map/ppermute | solution.py:33
  238.7 28.9 %collective-permute-start.44 = (bf16[48,1536]{1,0:T(8,128)(2,1)}, bf16[48,1536]{1,0:T(8,128)(2,1)S(1)}, u32[]{:S(2)}, u32[]{:S(2)}) collective-permute-start(bf16[48,1536]{1,0:T(8,128)(2,1)} %get-tuple-element.225), channel_id=1, source_target_pairs={{0,2},{2,0},{4,6},{6,4},{1,3},{3,1},{5,7},{7,5},{8,10},{10,8},{12,... | collective-permute-start | bytes 442376 | tf_op jit(solution)/shard_map/ppermute | solution.py:33
  242.5 25.1 %collective-permute-start.45 = (bf16[48,1536]{1,0:T(8,128)(2,1)}, bf16[48,1536]{1,0:T(8,128)(2,1)S(1)}, u32[]{:S(2)}, u32[]{:S(2)}) collective-permute-start(bf16[48,1536]{1,0:T(8,128)(2,1)} %copy-done.23), channel_id=1, source_target_pairs={{0,4},{2,6},{4,0},{6,2},{1,5},{3,7},{5,1},{7,3},{8,12},{10,14},{12... | collective-permute-start | bytes 442376 | tf_op jit(solution)/shard_map/ppermute | solution.py:33
  (72 other events, 711.6 us)
Sparse Core Ops, SparseCore 0:
  11.6 101.6 all-gather.1
